TPU v7x, 1024 devices: a whole 4x4x32 slice. The times are simulated.
1024 devices in a mesh: lat: 32 (over x, z_lo), lon: 32 (over z_hi, y, core).
Axes of the slice: x: 4, y: 4, z: 32 (z_hi: 4, z_lo: 8; z = z_hi * 8 + z_lo), core: 2. Of those that a mesh axis runs over, the one named last changes fastest.
Arguments:
- u_vel: float32 [4, 1024, 4096], P(None, 'lat', 'lon'), may hold values from -3 to 3
- v_vel: float32 [4, 1024, 4096], P(None, 'lat', 'lon'), may hold values from -3 to 3
- temp: float32 [4, 1024, 4096], P(None, 'lat', 'lon'), may hold values from -6 to 6
- salt: float32 [4, 1024, 4096], P(None, 'lat', 'lon'), may hold values from -6 to 6
- eta: float32 [1024, 4096], P('lat', 'lon'), may hold values from -5 to 5
- wet_levels: int32 [3, 1024, 4096], P(None, 'lat', 'lon'), may hold values from 0 to 4, as said below
Outputs:
- u_new: float32 [4, 1024, 4096], P(None, 'lat', 'lon')
- v_new: float32 [4, 1024, 4096], P(None, 'lat', 'lon')
- temp_new: float32 [4, 1024, 4096], P(None, 'lat', 'lon')
- salt_new: float32 [4, 1024, 4096], P(None, 'lat', 'lon')
- eta_new: float32 [1024, 4096], P('lat', 'lon')
Inputs may be any that keep to these rules, and one draw needn't show every extreme that they name: `wet_levels`: entry 0 of a column is its number of wet levels, 0 on land; entry 1 is the smaller of entry 0 of the column and of its eastern neighbour (periodic in longitude); entry 2 the smaller of entry 0 of the column and of its northern neighbour, 0 on the last row.
All inputs are finite; a program needn't handle non-finite values.
Results may differ from a plain program's by a relative error of at most 0.0003.
Values sent between devices are 32-bit elements; how exact they have to be, the bound alone decides.
A program may use at most 32 MiB of HBM per device.

v0:
```python
import jax
import jax.numpy as jnp
from jax import lax
from jax.sharding import PartitionSpec as P

SUB = 8


time_step = 0.4
epsilon = 1e-06
wave_share = 0.45


def padded_2(shard, sides, width):
    for axis, dim in sides:
        peers, length = (lax.axis_size(axis), shard.shape[dim])
        up = [(i, (i + 1) % peers) for i in range(peers)]
        down = [(j, i) for i, j in up]
        last = lax.slice_in_dim(shard, length - width, length, axis=dim)
        first = lax.slice_in_dim(shard, 0, width, axis=dim)
        before = lax.ppermute(last, axis, up)
        after = lax.ppermute(first, axis, down)
        shard = jnp.concatenate([before, shard, after], axis=dim)
    return shard


def shifted(shard, axis, by):
    peers = lax.axis_size(axis)
    return lax.ppermute(shard, axis, [(i, (i + by) % peers) for i in range(peers)])


def passed_along(shard, axis, by):
    peers = lax.axis_size(axis)
    pairs = [(i, i + by) for i in range(peers) if 0 <= i + by < peers]
    return lax.ppermute(shard, axis, pairs)


def weno_value(minus_two, minus_one, centre, plus_one, plus_two):
    first = (2.0 * minus_two - 7.0 * minus_one + 11.0 * centre) / 6.0
    second = (-minus_one + 5.0 * centre + 2.0 * plus_one) / 6.0
    third = (2.0 * centre + 5.0 * plus_one - plus_two) / 6.0
    rough_a = (
        13.0 / 12.0 * (minus_two - 2.0 * minus_one + centre) ** 2
        + 0.25 * (minus_two - 4.0 * minus_one + 3.0 * centre) ** 2
    )
    rough_b = (
        13.0 / 12.0 * (minus_one - 2.0 * centre + plus_one) ** 2
        + 0.25 * (minus_one - plus_one) ** 2
    )
    rough_c = (
        13.0 / 12.0 * (centre - 2.0 * plus_one + plus_two) ** 2
        + 0.25 * (3.0 * centre - 4.0 * plus_one + plus_two) ** 2
    )
    weight_a = 0.1 / (epsilon + rough_a) ** 2
    weight_b = 0.6 / (epsilon + rough_b) ** 2
    weight_c = 0.3 / (epsilon + rough_c) ** 2
    return (weight_a * first + weight_b * second + weight_c * third) / (
        weight_a + weight_b + weight_c
    )


def face_values(cells, flow, axis):
    axis = axis % cells.ndim
    count = cells.shape[axis] - 5
    pieces = [lax.slice_in_dim(cells, start, start + count, axis=axis) for start in range(6)]
    upwind = weno_value(pieces[0], pieces[1], pieces[2], pieces[3], pieces[4])
    downwind = weno_value(pieces[5], pieces[4], pieces[3], pieces[2], pieces[1])
    return jnp.where(flow >= 0.0, upwind, downwind)


def advect(fields, east, north):
    rows_y = fields.shape[-2] - 6
    cols_x = fields.shape[-1] - 6
    flow_x = east[..., 3 : 3 + rows_y, 2 : 3 + cols_x]
    flux_x = flow_x * face_values(fields[..., 3 : 3 + rows_y, :], flow_x, -1)
    flow_y = north[..., 2 : 3 + rows_y, 3 : 3 + cols_x]
    flux_y = flow_y * face_values(fields[..., :, 3 : 3 + cols_x], flow_y, -2)
    return -(flux_x[..., 1:] - flux_x[..., :-1] + (flux_y[..., 1:, :] - flux_y[..., :-1, :]))


def toward(values, axis, offset):
    length = values.shape[axis]
    blank = jnp.zeros_like(lax.slice_in_dim(values, 0, 1, axis=axis))
    if offset == 1:
        return jnp.concatenate([blank, lax.slice_in_dim(values, 0, length - 1, axis=axis)], axis)
    return jnp.concatenate([lax.slice_in_dim(values, 1, length, axis=axis), blank], axis)


def surface_run(state, statics, wave):
    height, trans_x, trans_y = (state[0], state[1], state[2])
    force_x, force_y, depth_x, depth_y = (statics[0], statics[1], statics[2], statics[3])
    height = height - (trans_x - toward(trans_x, 1, 1) + trans_y - toward(trans_y, 0, 1))
    trans_x = trans_x - wave * depth_x * (toward(height, 1, -1) - height) + force_x
    trans_y = trans_y - wave * depth_y * (toward(height, 0, -1) - height) + force_y
    return jnp.stack([height, trans_x, trans_y])


def close_poles(padded, width):
    count = lax.axis_size("lat")
    place = lax.axis_index("lat")
    rows = padded.shape[-2]
    row_ids = jnp.arange(rows)
    keep = ((row_ids >= width) | (place > 0)) & ((row_ids < rows - width) | (place < count - 1))
    return padded * keep.astype(padded.dtype)[:, None]


def on_device(u_vel, v_vel, temp, salt, eta, wet_levels):
    levels_k, rows_y, cols_x = u_vel.shape
    levels = wet_levels.astype(jnp.float32)
    depths = jnp.arange(levels_k, dtype=jnp.float32)[:, None, None]
    wet_c = (depths < levels[0]).astype(jnp.float32)
    wet_x = (depths < levels[1]).astype(jnp.float32)
    wet_y = (depths < levels[2]).astype(jnp.float32)
    east_flow = u_vel * wet_x
    north_flow = v_vel * wet_y
    temp_wet = temp * wet_c
    salt_wet = salt * wet_c
    padded_shape = (levels_k, rows_y + 6, cols_x + 6)
    moved = padded_2(
        jnp.concatenate([east_flow, north_flow, temp_wet, salt_wet]), (("lat", 1), ("lon", 2)), 3
    )
    every = close_poles(moved, 3).reshape((4,) + padded_shape)
    motion = every[:2]
    tracer_pad = every[2:]
    tendency = advect(motion, motion[0], motion[1])
    step_u = (east_flow + time_step * tendency[0]) * wet_x
    step_v = (north_flow + time_step * tendency[1]) * wet_y
    scale = time_step / SUB
    statics = jnp.stack(
        [
            scale * jnp.sum(tendency[0] * wet_x, 0),
            scale * jnp.sum(tendency[1] * wet_y, 0),
            levels[1],
            levels[2],
        ]
    )
    surface = jnp.stack([eta, jnp.sum(east_flow, 0), jnp.sum(north_flow, 0)])
    wave = wave_share / levels_k
    padded_statics = jnp.pad(statics, ((0, 0), (1, 1), (1, 1)))
    for repeat in range(SUB):
        moved = padded_2(surface, (("lat", 1), ("lon", 2)), 1)
        result = surface_run(close_poles(moved, 1), padded_statics, wave)
        surface = result[:, 1 : 1 + rows_y, 1 : 1 + cols_x]
    safe_x = jnp.maximum(levels[1], 1.0)
    safe_y = jnp.maximum(levels[2], 1.0)
    new_u = (step_u - jnp.sum(step_u, 0) / safe_x + surface[1] / safe_x) * wet_x
    new_v = (step_v - jnp.sum(step_v, 0) / safe_y + surface[2] / safe_y) * wet_y
    tracer_wet = jnp.stack([temp_wet, salt_wet])
    flux_x = new_u * face_values(tracer_pad[..., 3 : 3 + rows_y, 1:], new_u, -1)
    flux_y = new_v * face_values(tracer_pad[..., 1:, 3 : 3 + cols_x], new_v, -2)
    west_edge = shifted(flux_x[..., -1], "lon", 1)
    south_edge = passed_along(flux_y[..., -1, :], "lat", 1)
    before_x = jnp.concatenate([west_edge[..., None], flux_x[..., :-1]], -1)
    before_y = jnp.concatenate([south_edge[..., None, :], flux_y[..., :-1, :]], -2)
    tendency = -(flux_x - before_x + (flux_y - before_y))
    new_tracer = (tracer_wet + time_step * tendency) * wet_c
    return (new_u, new_v, new_tracer[0], new_tracer[1], surface[0])


def solution(mesh):
    in_specs = (
        P(None, "lat", "lon"),
        P(None, "lat", "lon"),
        P(None, "lat", "lon"),
        P(None, "lat", "lon"),
        P("lat", "lon"),
        P(None, "lat", "lon"),
    )
    out_specs = (
        P(None, "lat", "lon"),
        P(None, "lat", "lon"),
        P(None, "lat", "lon"),
        P(None, "lat", "lon"),
        P("lat", "lon"),
    )
    return jax.shard_map(
        on_device, mesh=mesh, in_specs=in_specs, out_specs=out_specs, check_vma=False
    )
```

profile of v0, /device:TPU:25, one launch (start us, length us, event | category | flops | bytes accessed | tf_op | source)
XLA Modules:
  0.0 378.4 jit_solution(14377544094738489855)
XLA Ops:
  3.3 15.1 %collective-permute-start.1 = (f32[16,3,128]{2,1,0:T(4,128)S(1)}, f32[16,3,128]{2,1,0:T(4,128)S(1)}, u32[]{:S(2)}, u32[]{:S(2)}) collective-permute-start(f32[16,3,128]{2,1,0:T(4,128)S(1)} %get-tuple-element.40), channel_id=1, source_target_pairs={{32,0},{64,32},{96,64},{128,96},{160,128},{192,160},{224,192},{256... | collective-permute-start | bytes 73736 | tf_op jit(solution)/shard_map/ppermute | solution.py:22
  20.3 11.4 %collective-permute-done = f32[16,3,128]{2,1,0:T(4,128)S(1)} collective-permute-done((f32[16,3,128]{2,1,0:T(4,128)S(1)}, f32[16,3,128]{2,1,0:T(4,128)S(1)}, u32[]{:S(2)}, u32[]{:S(2)}) %collective-permute-start) | collective-permute-done | bytes 24608 | tf_op jit(solution)/shard_map/ppermute | solution.py:21
  31.9 4.0 %collective-permute-start.3 = (f32[16,38,3]{2,1,0:T(8,128)S(1)}, f32[16,38,3]{2,1,0:T(8,128)S(1)}, u32[]{:S(2)}, u32[]{:S(2)}) collective-permute-start(f32[16,38,3]{2,1,0:T(8,128)S(1)} %get-tuple-element.38), channel_id=1, source_target_pairs={{1,0},{2,1},{3,2},{4,3},{5,4},{6,5},{7,6},{8,7},{9,8},{10,9},{11,1... | collective-permute-start | bytes 21896 | tf_op jit(solution)/shard_map/ppermute | solution.py:22
  35.9 19.9 %collective-permute-start.2 = (f32[16,38,3]{2,1,0:T(8,128)S(1)}, f32[16,38,3]{2,1,0:T(8,128)S(1)}, u32[]{:S(2)}, u32[]{:S(2)}) collective-permute-start(f32[16,38,3]{2,1,0:T(8,128)S(1)} %get-tuple-element.37), channel_id=1, source_target_pairs={{0,1},{1,2},{2,3},{3,4},{4,5},{5,6},{6,7},{7,8},{8,9},{9,10},{10,1... | collective-permute-start | bytes 21896 | tf_op jit(solution)/shard_map/ppermute | solution.py:21
  58.9 12.4 %collective-permute-done.2 = f32[16,38,3]{2,1,0:T(8,128)S(1)} collective-permute-done((f32[16,38,3]{2,1,0:T(8,128)S(1)}, f32[16,38,3]{2,1,0:T(8,128)S(1)}, u32[]{:S(2)}, u32[]{:S(2)}) %collective-permute-start.2) | collective-permute-done | bytes 7328 | tf_op jit(solution)/shard_map/ppermute | solution.py:21
  75.3 5.1 %collective-permute-start.5 = (f32[3,1,128]{2,1,0:T(1,128)S(1)}, f32[3,1,128]{2,1,0:T(1,128)S(1)}, u32[]{:S(2)}, u32[]{:S(2)}) collective-permute-start(f32[3,1,128]{2,1,0:T(1,128)S(1)} %get-tuple-element.80), channel_id=1, source_target_pairs={{32,0},{64,32},{96,64},{128,96},{160,128},{192,160},{224,192},{256... | collective-permute-start | bytes 4616 | tf_op jit(solution)/shard_map/ppermute | solution.py:22
  82.3 11.1 %collective-permute-done.4 = f32[3,1,128]{2,1,0:T(1,128)S(1)} collective-permute-done((f32[3,1,128]{2,1,0:T(1,128)S(1)}, f32[3,1,128]{2,1,0:T(1,128)S(1)}, u32[]{:S(2)}, u32[]{:S(2)}) %collective-permute-start.4) | collective-permute-done | bytes 1568 | tf_op jit(solution)/shard_map/ppermute | solution.py:21
  95.4 14.5 %collective-permute-start.6 = (f32[3,34,1]{2,1,0:T(8,128)S(1)}, f32[3,34,1]{2,1,0:T(8,128)S(1)}, u32[]{:S(2)}, u32[]{:S(2)}) collective-permute-start(f32[3,34,1]{2,1,0:T(8,128)S(1)} %get-tuple-element.73), channel_id=1, source_target_pairs={{0,1},{1,2},{2,3},{3,4},{4,5},{5,6},{6,7},{7,8},{8,9},{9,10},{10,1... | collective-permute-start | bytes 1232 | tf_op jit(solution)/shard_map/ppermute | solution.py:21
  117.0 9.6 %collective-permute-done.8 = f32[3,1,128]{2,1,0:T(1,128)S(1)} collective-permute-done((f32[3,1,128]{2,1,0:T(1,128)S(1)}, f32[3,1,128]{2,1,0:T(1,128)S(1)}, u32[]{:S(2)}, u32[]{:S(2)}) %collective-permute-start.8) | collective-permute-done | bytes 1568 | tf_op jit(solution)/shard_map/ppermute | solution.py:21
  128.6 16.8 %collective-permute-start.10 = (f32[3,34,1]{2,1,0:T(8,128)S(1)}, f32[3,34,1]{2,1,0:T(8,128)S(1)}, u32[]{:S(2)}, u32[]{:S(2)}) collective-permute-start(f32[3,34,1]{2,1,0:T(8,128)S(1)} %get-tuple-element.71), channel_id=1, source_target_pairs={{0,1},{1,2},{2,3},{3,4},{4,5},{5,6},{6,7},{7,8},{8,9},{9,10},{10,1... | collective-permute-start | bytes 1232 | tf_op jit(solution)/shard_map/ppermute | solution.py:21
  152.6 9.8 %collective-permute-done.12 = f32[3,1,128]{2,1,0:T(1,128)S(1)} collective-permute-done((f32[3,1,128]{2,1,0:T(1,128)S(1)}, f32[3,1,128]{2,1,0:T(1,128)S(1)}, u32[]{:S(2)}, u32[]{:S(2)}) %collective-permute-start.12) | collective-permute-done | bytes 1568 | tf_op jit(solution)/shard_map/ppermute | solution.py:21
  164.4 16.8 %collective-permute-start.14 = (f32[3,34,1]{2,1,0:T(8,128)S(1)}, f32[3,34,1]{2,1,0:T(8,128)S(1)}, u32[]{:S(2)}, u32[]{:S(2)}) collective-permute-start(f32[3,34,1]{2,1,0:T(8,128)S(1)} %get-tuple-element.69), channel_id=1, source_target_pairs={{0,1},{1,2},{2,3},{3,4},{4,5},{5,6},{6,7},{7,8},{8,9},{9,10},{10,1... | collective-permute-start | bytes 1232 | tf_op jit(solution)/shard_map/ppermute | solution.py:21
  188.3 9.6 %collective-permute-done.16 = f32[3,1,128]{2,1,0:T(1,128)S(1)} collective-permute-done((f32[3,1,128]{2,1,0:T(1,128)S(1)}, f32[3,1,128]{2,1,0:T(1,128)S(1)}, u32[]{:S(2)}, u32[]{:S(2)}) %collective-permute-start.16) | collective-permute-done | bytes 1568 | tf_op jit(solution)/shard_map/ppermute | solution.py:21
  199.9 16.4 %collective-permute-start.18 = (f32[3,34,1]{2,1,0:T(8,128)S(1)}, f32[3,34,1]{2,1,0:T(8,128)S(1)}, u32[]{:S(2)}, u32[]{:S(2)}) collective-permute-start(f32[3,34,1]{2,1,0:T(8,128)S(1)} %get-tuple-element.67), channel_id=1, source_target_pairs={{0,1},{1,2},{2,3},{3,4},{4,5},{5,6},{6,7},{7,8},{8,9},{9,10},{10,1... | collective-permute-start | bytes 1232 | tf_op jit(solution)/shard_map/ppermute | solution.py:21
  223.4 9.6 %collective-permute-done.20 = f32[3,1,128]{2,1,0:T(1,128)S(1)} collective-permute-done((f32[3,1,128]{2,1,0:T(1,128)S(1)}, f32[3,1,128]{2,1,0:T(1,128)S(1)}, u32[]{:S(2)}, u32[]{:S(2)}) %collective-permute-start.20) | collective-permute-done | bytes 1568 | tf_op jit(solution)/shard_map/ppermute | solution.py:21
  235.0 16.3 %collective-permute-start.22 = (f32[3,34,1]{2,1,0:T(8,128)S(1)}, f32[3,34,1]{2,1,0:T(8,128)S(1)}, u32[]{:S(2)}, u32[]{:S(2)}) collective-permute-start(f32[3,34,1]{2,1,0:T(8,128)S(1)} %get-tuple-element.65), channel_id=1, source_target_pairs={{0,1},{1,2},{2,3},{3,4},{4,5},{5,6},{6,7},{7,8},{8,9},{9,10},{10,1... | collective-permute-start | bytes 1232 | tf_op jit(solution)/shard_map/ppermute | solution.py:21
  255.0 3.4 collective-permute-start.24
  258.4 9.6 %collective-permute-done.24 = f32[3,1,128]{2,1,0:T(1,128)S(1)} collective-permute-done((f32[3,1,128]{2,1,0:T(1,128)S(1)}, f32[3,1,128]{2,1,0:T(1,128)S(1)}, u32[]{:S(2)}, u32[]{:S(2)}) %collective-permute-start.24) | collective-permute-done | bytes 1568 | tf_op jit(solution)/shard_map/ppermute | solution.py:21
  270.0 16.2 %collective-permute-start.26 = (f32[3,34,1]{2,1,0:T(8,128)S(1)}, f32[3,34,1]{2,1,0:T(8,128)S(1)}, u32[]{:S(2)}, u32[]{:S(2)}) collective-permute-start(f32[3,34,1]{2,1,0:T(8,128)S(1)} %get-tuple-element.63), channel_id=1, source_target_pairs={{0,1},{1,2},{2,3},{3,4},{4,5},{5,6},{6,7},{7,8},{8,9},{9,10},{10,1... | collective-permute-start | bytes 1232 | tf_op jit(solution)/shard_map/ppermute | solution.py:21
  293.4 9.6 %collective-permute-done.28 = f32[3,1,128]{2,1,0:T(1,128)S(1)} collective-permute-done((f32[3,1,128]{2,1,0:T(1,128)S(1)}, f32[3,1,128]{2,1,0:T(1,128)S(1)}, u32[]{:S(2)}, u32[]{:S(2)}) %collective-permute-start.28) | collective-permute-done | bytes 1568 | tf_op jit(solution)/shard_map/ppermute | solution.py:21
  305.0 16.2 %collective-permute-start.30 = (f32[3,34,1]{2,1,0:T(8,128)S(1)}, f32[3,34,1]{2,1,0:T(8,128)S(1)}, u32[]{:S(2)}, u32[]{:S(2)}) collective-permute-start(f32[3,34,1]{2,1,0:T(8,128)S(1)} %get-tuple-element.61), channel_id=1, source_target_pairs={{0,1},{1,2},{2,3},{3,4},{4,5},{5,6},{6,7},{7,8},{8,9},{9,10},{10,1... | collective-permute-start | bytes 1232 | tf_op jit(solution)/shard_map/ppermute | solution.py:21
  328.3 9.6 %collective-permute-done.32 = f32[3,1,128]{2,1,0:T(1,128)S(1)} collective-permute-done((f32[3,1,128]{2,1,0:T(1,128)S(1)}, f32[3,1,128]{2,1,0:T(1,128)S(1)}, u32[]{:S(2)}, u32[]{:S(2)}) %collective-permute-start.32) | collective-permute-done | bytes 1568 | tf_op jit(solution)/shard_map/ppermute | solution.py:21
  339.9 16.2 %collective-permute-start.34 = (f32[3,34,1]{2,1,0:T(8,128)S(1)}, f32[3,34,1]{2,1,0:T(8,128)S(1)}, u32[]{:S(2)}, u32[]{:S(2)}) collective-permute-start(f32[3,34,1]{2,1,0:T(8,128)S(1)} %get-tuple-element.59), channel_id=1, source_target_pairs={{0,1},{1,2},{2,3},{3,4},{4,5},{5,6},{6,7},{7,8},{8,9},{9,10},{10,1... | collective-permute-start | bytes 1232 | tf_op jit(solution)/shard_map/ppermute | solution.py:21
  360.3 15.1 %collective-permute-start.36 = (f32[2,4,32]{2,1,0:T(4,128)S(1)}, f32[2,4,32]{2,1,0:T(4,128)S(1)}, u32[]{:S(2)}, u32[]{:S(2)}) collective-permute-start(f32[2,4,32]{2,1,0:T(4,128)S(1)} %slice_reduce_fusion), channel_id=1, source_target_pairs={{0,1},{1,2},{2,3},{3,4},{4,5},{5,6},{6,7},{7,8},{8,9},{9,10},{10,1... | collective-permute-start | bytes 3080 | tf_op jit(solution)/shard_map/ppermute | solution.py:29
  (191 shorter events, 82.5 us)
Async XLA Ops:
  3.3 17.0 %collective-permute-start.1 = (f32[16,3,128]{2,1,0:T(4,128)S(1)}, f32[16,3,128]{2,1,0:T(4,128)S(1)}, u32[]{:S(2)}, u32[]{:S(2)}) collective-permute-start(f32[16,3,128]{2,1,0:T(4,128)S(1)} %get-tuple-element.40), channel_id=1, source_target_pairs={{32,0},{64,32},{96,64},{128,96},{160,128},{192,160},{224,192},{256... | collective-permute-start | bytes 73736 | tf_op jit(solution)/shard_map/ppermute | solution.py:22
  18.3 13.4 %collective-permute-start = (f32[16,3,128]{2,1,0:T(4,128)S(1)}, f32[16,3,128]{2,1,0:T(4,128)S(1)}, u32[]{:S(2)}, u32[]{:S(2)}) collective-permute-start(f32[16,3,128]{2,1,0:T(4,128)S(1)} %get-tuple-element.39), channel_id=1, source_target_pairs={{0,32},{32,64},{64,96},{96,128},{128,160},{160,192},{192,224},{224... | collective-permute-start | bytes 73736 | tf_op jit(solution)/shard_map/ppermute | solution.py:21
  31.9 27.0 %collective-permute-start.3 = (f32[16,38,3]{2,1,0:T(8,128)S(1)}, f32[16,38,3]{2,1,0:T(8,128)S(1)}, u32[]{:S(2)}, u32[]{:S(2)}) collective-permute-start(f32[16,38,3]{2,1,0:T(8,128)S(1)} %get-tuple-element.38), channel_id=1, source_target_pairs={{1,0},{2,1},{3,2},{4,3},{5,4},{6,5},{7,6},{8,7},{9,8},{10,9},{11,1... | collective-permute-start | bytes 21896 | tf_op jit(solution)/shard_map/ppermute | solution.py:22
  35.9 35.4 %collective-permute-start.2 = (f32[16,38,3]{2,1,0:T(8,128)S(1)}, f32[16,38,3]{2,1,0:T(8,128)S(1)}, u32[]{:S(2)}, u32[]{:S(2)}) collective-permute-start(f32[16,38,3]{2,1,0:T(8,128)S(1)} %get-tuple-element.37), channel_id=1, source_target_pairs={{0,1},{1,2},{2,3},{3,4},{4,5},{5,6},{6,7},{7,8},{8,9},{9,10},{10,1... | collective-permute-start | bytes 21896 | tf_op jit(solution)/shard_map/ppermute | solution.py:21
  80.4 13.0 %collective-permute-start.4 = (f32[3,1,128]{2,1,0:T(1,128)S(1)}, f32[3,1,128]{2,1,0:T(1,128)S(1)}, u32[]{:S(2)}, u32[]{:S(2)}) collective-permute-start(f32[3,1,128]{2,1,0:T(1,128)S(1)} %get-tuple-element.79), channel_id=1, source_target_pairs={{0,32},{32,64},{64,96},{96,128},{128,160},{160,192},{192,224},{224... | collective-permute-start | bytes 4616 | tf_op jit(solution)/shard_map/ppermute | solution.py:21
  93.5 16.5 %collective-permute-start.7 = (f32[3,34,1]{2,1,0:T(8,128)S(1)}, f32[3,34,1]{2,1,0:T(8,128)S(1)}, u32[]{:S(2)}, u32[]{:S(2)}) collective-permute-start(f32[3,34,1]{2,1,0:T(8,128)S(1)} %get-tuple-element.74), channel_id=1, source_target_pairs={{1,0},{2,1},{3,2},{4,3},{5,4},{6,5},{7,6},{8,7},{9,8},{10,9},{11,1... | collective-permute-start | bytes 1232 | tf_op jit(solution)/shard_map/ppermute | solution.py:22
  95.4 15.7 %collective-permute-start.6 = (f32[3,34,1]{2,1,0:T(8,128)S(1)}, f32[3,34,1]{2,1,0:T(8,128)S(1)}, u32[]{:S(2)}, u32[]{:S(2)}) collective-permute-start(f32[3,34,1]{2,1,0:T(8,128)S(1)} %get-tuple-element.73), channel_id=1, source_target_pairs={{0,1},{1,2},{2,3},{3,4},{4,5},{5,6},{6,7},{7,8},{8,9},{9,10},{10,1... | collective-permute-start | bytes 1232 | tf_op jit(solution)/shard_map/ppermute | solution.py:21
  113.6 13.0 %collective-permute-start.8 = (f32[3,1,128]{2,1,0:T(1,128)S(1)}, f32[3,1,128]{2,1,0:T(1,128)S(1)}, u32[]{:S(2)}, u32[]{:S(2)}) collective-permute-start(f32[3,1,128]{2,1,0:T(1,128)S(1)} %get-tuple-element.57), channel_id=1, source_target_pairs={{0,32},{32,64},{64,96},{96,128},{128,160},{160,192},{192,224},{224... | collective-permute-start | bytes 4616 | tf_op jit(solution)/shard_map/ppermute | solution.py:21
  126.7 18.8 %collective-permute-start.11 = (f32[3,34,1]{2,1,0:T(8,128)S(1)}, f32[3,34,1]{2,1,0:T(8,128)S(1)}, u32[]{:S(2)}, u32[]{:S(2)}) collective-permute-start(f32[3,34,1]{2,1,0:T(8,128)S(1)} %get-tuple-element.72), channel_id=1, source_target_pairs={{1,0},{2,1},{3,2},{4,3},{5,4},{6,5},{7,6},{8,7},{9,8},{10,9},{11,1... | collective-permute-start | bytes 1232 | tf_op jit(solution)/shard_map/ppermute | solution.py:22
  128.6 18.1 %collective-permute-start.10 = (f32[3,34,1]{2,1,0:T(8,128)S(1)}, f32[3,34,1]{2,1,0:T(8,128)S(1)}, u32[]{:S(2)}, u32[]{:S(2)}) collective-permute-start(f32[3,34,1]{2,1,0:T(8,128)S(1)} %get-tuple-element.71), channel_id=1, source_target_pairs={{0,1},{1,2},{2,3},{3,4},{4,5},{5,6},{6,7},{7,8},{8,9},{9,10},{10,1... | collective-permute-start | bytes 1232 | tf_op jit(solution)/shard_map/ppermute | solution.py:21
  162.5 18.7 %collective-permute-start.15 = (f32[3,34,1]{2,1,0:T(8,128)S(1)}, f32[3,34,1]{2,1,0:T(8,128)S(1)}, u32[]{:S(2)}, u32[]{:S(2)}) collective-permute-start(f32[3,34,1]{2,1,0:T(8,128)S(1)} %get-tuple-element.70), channel_id=1, source_target_pairs={{1,0},{2,1},{3,2},{4,3},{5,4},{6,5},{7,6},{8,7},{9,8},{10,9},{11,1... | collective-permute-start | bytes 1232 | tf_op jit(solution)/shard_map/ppermute | solution.py:22
  164.4 18.1 %collective-permute-start.14 = (f32[3,34,1]{2,1,0:T(8,128)S(1)}, f32[3,34,1]{2,1,0:T(8,128)S(1)}, u32[]{:S(2)}, u32[]{:S(2)}) collective-permute-start(f32[3,34,1]{2,1,0:T(8,128)S(1)} %get-tuple-element.69), channel_id=1, source_target_pairs={{0,1},{1,2},{2,3},{3,4},{4,5},{5,6},{6,7},{7,8},{8,9},{9,10},{10,1... | collective-permute-start | bytes 1232 | tf_op jit(solution)/shard_map/ppermute | solution.py:21
  198.0 18.3 %collective-permute-start.19 = (f32[3,34,1]{2,1,0:T(8,128)S(1)}, f32[3,34,1]{2,1,0:T(8,128)S(1)}, u32[]{:S(2)}, u32[]{:S(2)}) collective-permute-start(f32[3,34,1]{2,1,0:T(8,128)S(1)} %get-tuple-element.68), channel_id=1, source_target_pairs={{1,0},{2,1},{3,2},{4,3},{5,4},{6,5},{7,6},{8,7},{9,8},{10,9},{11,1... | collective-permute-start | bytes 1232 | tf_op jit(solution)/shard_map/ppermute | solution.py:22
  199.9 17.7 %collective-permute-start.18 = (f32[3,34,1]{2,1,0:T(8,128)S(1)}, f32[3,34,1]{2,1,0:T(8,128)S(1)}, u32[]{:S(2)}, u32[]{:S(2)}) collective-permute-start(f32[3,34,1]{2,1,0:T(8,128)S(1)} %get-tuple-element.67), channel_id=1, source_target_pairs={{0,1},{1,2},{2,3},{3,4},{4,5},{5,6},{6,7},{7,8},{8,9},{9,10},{10,1... | collective-permute-start | bytes 1232 | tf_op jit(solution)/shard_map/ppermute | solution.py:21
  220.0 13.0 %collective-permute-start.20 = (f32[3,1,128]{2,1,0:T(1,128)S(1)}, f32[3,1,128]{2,1,0:T(1,128)S(1)}, u32[]{:S(2)}, u32[]{:S(2)}) collective-permute-start(f32[3,1,128]{2,1,0:T(1,128)S(1)} %get-tuple-element.51), channel_id=1, source_target_pairs={{0,32},{32,64},{64,96},{96,128},{128,160},{160,192},{192,224},{224... | collective-permute-start | bytes 4616 | tf_op jit(solution)/shard_map/ppermute | solution.py:21
  233.1 18.2 %collective-permute-start.23 = (f32[3,34,1]{2,1,0:T(8,128)S(1)}, f32[3,34,1]{2,1,0:T(8,128)S(1)}, u32[]{:S(2)}, u32[]{:S(2)}) collective-permute-start(f32[3,34,1]{2,1,0:T(8,128)S(1)} %get-tuple-element.66), channel_id=1, source_target_pairs={{1,0},{2,1},{3,2},{4,3},{5,4},{6,5},{7,6},{8,7},{9,8},{10,9},{11,1... | collective-permute-start | bytes 1232 | tf_op jit(solution)/shard_map/ppermute | solution.py:22
  235.0 17.6 %collective-permute-start.22 = (f32[3,34,1]{2,1,0:T(8,128)S(1)}, f32[3,34,1]{2,1,0:T(8,128)S(1)}, u32[]{:S(2)}, u32[]{:S(2)}) collective-permute-start(f32[3,34,1]{2,1,0:T(8,128)S(1)} %get-tuple-element.65), channel_id=1, source_target_pairs={{0,1},{1,2},{2,3},{3,4},{4,5},{5,6},{6,7},{7,8},{8,9},{9,10},{10,1... | collective-permute-start | bytes 1232 | tf_op jit(solution)/shard_map/ppermute | solution.py:21
  268.1 18.2 %collective-permute-start.27 = (f32[3,34,1]{2,1,0:T(8,128)S(1)}, f32[3,34,1]{2,1,0:T(8,128)S(1)}, u32[]{:S(2)}, u32[]{:S(2)}) collective-permute-start(f32[3,34,1]{2,1,0:T(8,128)S(1)} %get-tuple-element.64), channel_id=1, source_target_pairs={{1,0},{2,1},{3,2},{4,3},{5,4},{6,5},{7,6},{8,7},{9,8},{10,9},{11,1... | collective-permute-start | bytes 1232 | tf_op jit(solution)/shard_map/ppermute | solution.py:22
  270.0 17.5 %collective-permute-start.26 = (f32[3,34,1]{2,1,0:T(8,128)S(1)}, f32[3,34,1]{2,1,0:T(8,128)S(1)}, u32[]{:S(2)}, u32[]{:S(2)}) collective-permute-start(f32[3,34,1]{2,1,0:T(8,128)S(1)} %get-tuple-element.63), channel_id=1, source_target_pairs={{0,1},{1,2},{2,3},{3,4},{4,5},{5,6},{6,7},{7,8},{8,9},{9,10},{10,1... | collective-permute-start | bytes 1232 | tf_op jit(solution)/shard_map/ppermute | solution.py:21
  303.1 18.2 %collective-permute-start.31 = (f32[3,34,1]{2,1,0:T(8,128)S(1)}, f32[3,34,1]{2,1,0:T(8,128)S(1)}, u32[]{:S(2)}, u32[]{:S(2)}) collective-permute-start(f32[3,34,1]{2,1,0:T(8,128)S(1)} %get-tuple-element.62), channel_id=1, source_target_pairs={{1,0},{2,1},{3,2},{4,3},{5,4},{6,5},{7,6},{8,7},{9,8},{10,9},{11,1... | collective-permute-start | bytes 1232 | tf_op jit(solution)/shard_map/ppermute | solution.py:22
  305.0 17.5 %collective-permute-start.30 = (f32[3,34,1]{2,1,0:T(8,128)S(1)}, f32[3,34,1]{2,1,0:T(8,128)S(1)}, u32[]{:S(2)}, u32[]{:S(2)}) collective-permute-start(f32[3,34,1]{2,1,0:T(8,128)S(1)} %get-tuple-element.61), channel_id=1, source_target_pairs={{0,1},{1,2},{2,3},{3,4},{4,5},{5,6},{6,7},{7,8},{8,9},{9,10},{10,1... | collective-permute-start | bytes 1232 | tf_op jit(solution)/shard_map/ppermute | solution.py:21
  338.0 18.2 %collective-permute-start.35 = (f32[3,34,1]{2,1,0:T(8,128)S(1)}, f32[3,34,1]{2,1,0:T(8,128)S(1)}, u32[]{:S(2)}, u32[]{:S(2)}) collective-permute-start(f32[3,34,1]{2,1,0:T(8,128)S(1)} %get-tuple-element.60), channel_id=1, source_target_pairs={{1,0},{2,1},{3,2},{4,3},{5,4},{6,5},{7,6},{8,7},{9,8},{10,9},{11,1... | collective-permute-start | bytes 1232 | tf_op jit(solution)/shard_map/ppermute | solution.py:22
  339.9 17.5 %collective-permute-start.34 = (f32[3,34,1]{2,1,0:T(8,128)S(1)}, f32[3,34,1]{2,1,0:T(8,128)S(1)}, u32[]{:S(2)}, u32[]{:S(2)}) collective-permute-start(f32[3,34,1]{2,1,0:T(8,128)S(1)} %get-tuple-element.59), channel_id=1, source_target_pairs={{0,1},{1,2},{2,3},{3,4},{4,5},{5,6},{6,7},{7,8},{8,9},{9,10},{10,1... | collective-permute-start | bytes 1232 | tf_op jit(solution)/shard_map/ppermute | solution.py:21
  360.3 17.1 %collective-permute-start.36 = (f32[2,4,32]{2,1,0:T(4,128)S(1)}, f32[2,4,32]{2,1,0:T(4,128)S(1)}, u32[]{:S(2)}, u32[]{:S(2)}) collective-permute-start(f32[2,4,32]{2,1,0:T(4,128)S(1)} %slice_reduce_fusion), channel_id=1, source_target_pairs={{0,1},{1,2},{2,3},{3,4},{4,5},{5,6},{6,7},{7,8},{8,9},{9,10},{10,1... | collective-permute-start | bytes 3080 | tf_op jit(solution)/shard_map/ppermute | solution.py:29
  (24 other events, 191.4 us)
where the time goes:
time: 380 us; the launch traced here: 378 us
  starting transfers between devices  246 us (65%)
  waiting for transfers between devices  115 us (30%)
  other arithmetic  8.8 us (2%)
  local copies, waits for them, and re-layouts  6.56 us (2%)
    ppermute x18, starting transfers between devices, padded_2(): before = lax.ppermute(last, axis, up)  176 us
    ppermute x18, waiting for transfers between devices, padded_2(): before = lax.ppermute(last, axis, up)  112 us
    ppermute x18, starting transfers between devices, padded_2(): after = lax.ppermute(first, axis, down)  53.2 us
    ppermute x1, starting transfers between devices, shifted(): lax.ppermute(shard, axis, [(i, (i + by) % peers) for i in range(peers)])  15.1 us
  transfers between devices with their start and end apart: 38, of which 19 were waited for; matrix products, arithmetic and copies ran while one was open for 0% of the time, Pallas kernels for 0%

commit v1 on v0

v1 whole, which is shorter than its diff:
```python
import jax
import jax.numpy as jnp
from jax import lax
from jax.experimental import pallas as pl
from jax.experimental.pallas import tpu as pltpu
from jax.sharding import PartitionSpec as P

MESH = pl.DeviceIdType.MESH
F32 = jnp.float32
LEVELS = 4
SUB = 8
STEP = 0.4
WAVE = 0.45 / 4
EPS = 1e-6 * 12.0 / 13.0
ROWS = 32
COLS = 128
PAD = 16
EXT = ROWS + 2 * PAD
LO = 8
SPAN = 48

U_MAIN, V_MAIN, U_SW, U_SE, V_SW, V_SE = 0, 4, 8, 9, 10, 11


def lanes(x, shift):
    shift = shift % COLS
    return x if shift == 0 else pltpu.roll(x, shift, 1)


def rows(x, shift):
    return pltpu.roll(x, shift % x.shape[0], 0)


def correction(d0, d1, d2, d3):
    x0 = d1 - d0
    x1 = d2 - d1
    x2 = d3 - d2
    m1 = d1 + d1
    m2 = d2 + d2
    y0 = x0 + m1
    y1 = d1 + d2
    y2 = x2 - m2
    e0 = x0 * x0 + (y0 * y0) * (3.0 / 13.0) + EPS
    e1 = x1 * x1 + (y1 * y1) * (3.0 / 13.0) + EPS
    e2 = x2 * x2 + (y2 * y2) * (3.0 / 13.0) + EPS
    a0 = e1 * e2
    a1 = e0 * e2
    a2 = e0 * e1
    w0 = a0 * a0
    w1 = (a1 * a1) * 6.0
    w2 = (a2 * a2) * 3.0
    top = w0 * (5.0 * d1 - 2.0 * d0) + w1 * (d1 + m2) + w2 * (4.0 * d2 - d3)
    return top / ((w0 + w1 + w2) * 6.0)


def upwind_value(flow, q0, q1, gm2, gm1, g0, g1, g2):
    ahead = flow >= 0.0
    fix = correction(jnp.where(ahead, gm2, g2), jnp.where(ahead, gm1, g1), g0, jnp.where(ahead, g1, gm1))
    return jnp.where(ahead, q0 + fix, q1 - fix)


def x_parts(q):
    q1 = lanes(q, -1)
    g = q1 - q
    return q, q1, lanes(g, 2), lanes(g, 1), g, lanes(g, -1), lanes(g, -2)


def y_parts(ref, k, r0, n):
    q = [ref[k, pl.ds(r0 + s, n), :] for s in range(-2, 4)]
    g = [q[i + 1] - q[i] for i in range(5)]
    return q[2], q[3], g[0], g[1], g[2], g[3], g[4]


def ring(parts):
    lane = lax.broadcasted_iota(jnp.int32, parts[0].shape, 1)
    out = lanes(parts[0], 16)
    for k in range(1, LEVELS):
        out = jnp.where(lane >= 32 * k, lanes(parts[k], 32 * k + 16), out)
    return out


def level_sum(x):
    y = x + lanes(x, 64)
    return y + lanes(y, 32)


def spread(x, start):
    lane = lax.broadcasted_iota(jnp.int32, x.shape, 1)
    return level_sum(jnp.where((lane >= start) & (lane < start + 32), x, 0.0))


def kernel(n_lat, n_lon, u_hbm, v_hbm, t_hbm, s_hbm, e_hbm, w_hbm,
           u_out, v_out, t_out, s_out, e_out,
           raw, raw2, wet, UV, TS, WE, PK, TE, TW, RW, RE, RTW, RTE,
           TEND, FY, XU, XD, YU, YD, NV, NU, XS,
           in_sem, send_sem, recv_sem):
    lat = lax.axis_index("lat")
    lon = lax.axis_index("lon")
    north = (lax.rem(lat + 1, n_lat), lon)
    south = (lax.rem(lat + n_lat - 1, n_lat), lon)
    east = (lat, lax.rem(lon + 1, n_lon))
    west = (lat, lax.rem(lon + n_lon - 1, n_lon))

    barrier = pltpu.get_barrier_semaphore()
    for peer in (north, south, east, west):
        pl.semaphore_signal(barrier, inc=1, device_id=peer, device_id_type=MESH)

    loads = [
        pltpu.make_async_copy(w_hbm, wet, in_sem.at[0]),
        pltpu.make_async_copy(u_hbm, raw.at[pl.ds(0, 4)], in_sem.at[1]),
        pltpu.make_async_copy(v_hbm, raw.at[pl.ds(4, 4)], in_sem.at[2]),
        pltpu.make_async_copy(t_hbm, raw.at[pl.ds(8, 4)], in_sem.at[3]),
        pltpu.make_async_copy(s_hbm, raw.at[pl.ds(12, 4)], in_sem.at[4]),
        pltpu.make_async_copy(e_hbm, raw2, in_sem.at[5]),
    ]
    for load in loads:
        load.start()
    for load in loads:
        load.wait()

    OWN = pl.ds(PAD, ROWS)
    for k in range(LEVELS):
        UV[U_MAIN + k, OWN, :] = jnp.where(wet[1] > k, raw[k], 0.0)
        UV[V_MAIN + k, OWN, :] = jnp.where(wet[2] > k, raw[4 + k], 0.0)
        TS[k, OWN, :] = jnp.where(wet[0] > k, raw[8 + k], 0.0)
        TS[4 + k, OWN, :] = jnp.where(wet[0] > k, raw[12 + k], 0.0)
    WE[0, OWN, :] = wet[0].astype(F32)
    WE[1, OWN, :] = raw2[...]

    lane32 = lax.broadcasted_iota(jnp.int32, (ROWS, COLS), 1)
    half32 = lax.rem(lane32, 32) < 16
    ring_u = ring([UV[U_MAIN + k, OWN, :] for k in range(LEVELS)])
    ring_v = ring([UV[V_MAIN + k, OWN, :] for k in range(LEVELS)])
    PK[0, OWN, :] = jnp.where(half32, ring_u, lanes(ring_v, 16))
    PK[1, OWN, :] = jnp.where(lane32 < 32, lanes(raw2[...], 16), lanes(wet[0].astype(F32), 48))
    PK[2, OWN, :] = jnp.where(half32, lanes(ring_u, -16), ring_v)
    ring_t = ring([TS[k, OWN, :] for k in range(LEVELS)])
    ring_s = ring([TS[4 + k, OWN, :] for k in range(LEVELS)])
    TE[...] = jnp.where(half32, ring_t, lanes(ring_s, 16))
    TW[...] = jnp.where(half32, lanes(ring_t, -16), ring_s)

    pl.semaphore_wait(barrier, 4)

    def send(slot, src, dst, peer):
        copy = pltpu.make_async_remote_copy(
            src_ref=src, dst_ref=dst, send_sem=send_sem.at[slot], recv_sem=recv_sem.at[slot],
            device_id=peer, device_id_type=MESH)
        copy.start()
        return copy

    top, bottom = pl.ds(32, 16), pl.ds(16, 16)
    under, over = pl.ds(0, 16), pl.ds(48, 16)
    every = pl.ds(0, 8)
    corner_n = send(0, PK.at[:, top, :], PK.at[:, under, :], north)
    corner_s = send(1, PK.at[:, bottom, :], PK.at[:, over, :], south)
    bulk = [
        send(2, UV.at[every, top, :], UV.at[every, under, :], north),
        send(3, UV.at[every, bottom, :], UV.at[every, over, :], south),
        send(4, WE.at[:, top, :], WE.at[:, under, :], north),
        send(5, WE.at[:, bottom, :], WE.at[:, over, :], south),
        send(6, TS.at[:, pl.ds(40, 8), :], TS.at[:, pl.ds(8, 8), :], north),
        send(7, TS.at[:, pl.ds(16, 8), :], TS.at[:, pl.ds(48, 8), :], south),
    ]
    sides = [
        send(8, PK.at[pl.ds(0, 2), OWN, :], RW.at[:, OWN, :], east),
        send(9, PK.at[pl.ds(1, 2), OWN, :], RE.at[:, OWN, :], west),
        send(10, TE, RTW, east),
        send(11, TW, RTE, west),
    ]
    corner_n.wait_recv()
    relays = [
        send(12, PK.at[pl.ds(0, 2), under, :], RW.at[:, under, :], east),
        send(13, PK.at[pl.ds(1, 2), under, :], RE.at[:, under, :], west),
    ]
    corner_s.wait_recv()
    relays += [
        send(14, PK.at[pl.ds(0, 2), over, :], RW.at[:, over, :], east),
        send(15, PK.at[pl.ds(1, 2), over, :], RE.at[:, over, :], west),
    ]

    def tracer_x(k, carry):
        for r0 in range(0, ROWS, 16):
            q0, q1, gm2, gm1, g0, g1, g2 = x_parts(TS[k, pl.ds(PAD + r0, 16), :])
            XU[k, pl.ds(r0, 16), :] = q0 + correction(gm2, gm1, g0, g1)
            XD[k, pl.ds(r0, 16), :] = q1 - correction(g2, g1, g0, gm1)
        return carry

    lax.fori_loop(0, 8, tracer_x, 0)

    for copy in bulk:
        copy.wait_recv()

    zero16 = jnp.zeros((16, COLS), F32)
    FY[pl.ds(SPAN, 8), :] = jnp.zeros((8, COLS), F32)

    @pl.when(lat == 0)
    def _():
        for k in range(8):
            UV[k, under, :] = zero16
            TS[k, under, :] = zero16
        WE[0, under, :] = zero16
        WE[1, under, :] = zero16

    @pl.when(lat == n_lat - 1)
    def _():
        for k in range(8):
            UV[k, over, :] = zero16
            TS[k, over, :] = zero16
        WE[0, over, :] = zero16
        WE[1, over, :] = zero16

    def tendency(q_plane, u_plane, v_plane, out):
        for r0 in range(0, SPAN, 8):
            base = LO - 1 + r0
            FY[pl.ds(r0, 8), :] = UV[v_plane, pl.ds(base, 8), :] * upwind_value(
                UV[v_plane, pl.ds(base, 8), :], *y_parts(UV, q_plane, base, 8))
        for r0 in range(0, SPAN, 16):
            flow = UV[u_plane, pl.ds(LO + r0, 16), :]
            flux = flow * upwind_value(flow, *x_parts(UV[q_plane, pl.ds(LO + r0, 16), :]))
            TEND[out, pl.ds(r0, 16), :] = -(flux - lanes(flux, 1) + (
                FY[pl.ds(r0 + 1, 16), :] - FY[pl.ds(r0, 16), :]))

    def momentum(k, carry):
        tendency(k, k, V_MAIN + k, k)
        tendency(V_MAIN + k, k, V_MAIN + k, V_MAIN + k)
        return carry

    lax.fori_loop(0, LEVELS, momentum, 0)

    def tracer_y(k, carry):
        for r0 in range(0, 40, 8):
            q0, q1, gm2, gm1, g0, g1, g2 = y_parts(TS, k, PAD - 1 + r0, 8)
            YU[k, pl.ds(r0, 8), :] = q0 + correction(gm2, gm1, g0, g1)
            YD[k, pl.ds(r0, 8), :] = q1 - correction(g2, g1, g0, gm1)
        return carry

    lax.fori_loop(0, 8, tracer_y, 0)

    for copy in sides + relays:
        copy.wait_recv()

    @pl.when(lat == 0)
    def _():
        for i in range(2):
            RW[i, under, :] = zero16
            RE[i, under, :] = zero16

    @pl.when(lat == n_lat - 1)
    def _():
        for i in range(2):
            RW[i, over, :] = zero16
            RE[i, over, :] = zero16

    lane64 = lax.broadcasted_iota(jnp.int32, (EXT, COLS), 1)
    half = lax.rem(lane64, 32) < 16
    ring_u = ring([UV[U_MAIN + k] for k in range(LEVELS)])
    ring_v = ring([UV[V_MAIN + k] for k in range(LEVELS)])
    UV[U_SW] = jnp.where(half, RW[0], ring_u)
    UV[V_SW] = jnp.where(half, lanes(RW[0], -16), ring_v)
    UV[U_SE] = jnp.where(half, ring_u, lanes(RE[1], 16))
    UV[V_SE] = jnp.where(half, ring_v, RE[1])

    def strips(i, carry):
        tendency(U_SW + i, U_SW + i, V_SW + i, U_SW + i)
        tendency(V_SW + i, U_SW + i, V_SW + i, V_SW + i)
        return carry

    lax.fori_loop(0, 2, strips, 0)

    own_2d = jnp.where(lane64 < 32, lanes(WE[1], 16), lanes(WE[0], 48))
    west_2d = jnp.where(half, RW[1], own_2d)
    east_2d = jnp.where(half, own_2d, RE[0])
    lane = lax.broadcasted_iota(jnp.int32, (SPAN, COLS), 1)
    level = (lane // 32).astype(F32)
    BAND = pl.ds(LO, SPAN)

    def band(x):
        return x[LO:LO + SPAN]

    def joined(sw, main, se):
        return jnp.where(lane < 24, sw, jnp.where(lane < 64, lanes(main, 16), jnp.where(lane < 104, lanes(main, -16), se)))

    def shifted_up(x):
        return rows(x, -1)

    wet_sw = spread(west_2d, 32)
    wet_se = spread(east_2d, 32)
    wet_main = WE[0]
    eta_main = WE[1, BAND, :]
    eta_side = joined(spread(band(west_2d), 0), eta_main, spread(band(east_2d), 0))

    def faces(w):
        here = band(w)
        return jnp.minimum(here, lanes(here, -1)), jnp.minimum(here, band(shifted_up(w)))

    wx_main, wy_main = faces(wet_main)
    wx_sw, wy_sw = faces(wet_sw)
    wx_se, wy_se = faces(wet_se)
    wx_side = joined(wx_sw, wx_main, wx_se)
    wy_side = joined(wy_sw, wy_main, wy_se)

    def main_sum(ref, first, where_rows, limit=None):
        total = None
        for k in range(LEVELS):
            term = ref[first + k, where_rows, :]
            if limit is not None:
                term = jnp.where(limit > k, term, 0.0)
            total = term if total is None else total + term
        return total

    def side_sum(ref, plane, where_rows, limit=None):
        term = ref[plane, where_rows, :]
        if limit is not None:
            term = jnp.where(limit > level, term, 0.0)
        return level_sum(term)

    ALL = pl.ds(0, SPAN)
    scale = STEP / SUB
    push_x = main_sum(TEND, U_MAIN, ALL, wx_main)
    push_y = main_sum(TEND, V_MAIN, ALL, wy_main)
    push_x_sw = side_sum(TEND, U_SW, ALL, wx_sw)
    push_x_se = side_sum(TEND, U_SE, ALL, wx_se)
    push_y_sw = side_sum(TEND, V_SW, ALL, wy_sw)
    push_y_se = side_sum(TEND, V_SE, ALL, wy_se)
    tx0 = main_sum(UV, U_MAIN, BAND)
    ty0 = main_sum(UV, V_MAIN, BAND)
    tx0_sw, tx0_se = side_sum(UV, U_SW, BAND), side_sum(UV, U_SE, BAND)
    ty0_sw, ty0_se = side_sum(UV, V_SW, BAND), side_sum(UV, V_SE, BAND)
    LOWER = pl.ds(LO - 1, SPAN)
    tym_main = main_sum(UV, V_MAIN, LOWER)
    tym_side = joined(side_sum(UV, V_SW, LOWER), tym_main, side_sum(UV, V_SE, LOWER))

    def substeps(height, tx, ty, tym, fx, fy, cx, cy):
        for n in range(SUB):
            below = tym if n == 0 else rows(ty, 1)
            height = height - (tx - lanes(tx, 1) + ty - below)
            tx = tx - cx * (lanes(height, -1) - height) + fx
            ty = ty - cy * (rows(height, -1) - height) + fy
        return height, tx, ty

    h_main, tx_main, ty_main = substeps(
        eta_main, tx0, ty0, tym_main, scale * push_x, scale * push_y, WAVE * wx_main, WAVE * wy_main)
    h_side, tx_side, ty_side = substeps(
        eta_side, joined(tx0_sw, tx0, tx0_se), joined(ty0_sw, ty0, ty0_se), tym_side,
        scale * joined(push_x_sw, push_x, push_x_se), scale * joined(push_y_sw, push_y, push_y_se),
        WAVE * wx_side, WAVE * wy_side)

    own = slice(PAD - LO, PAD - LO + ROWS)
    e_out[...] = jnp.where(lane < 16, lanes(h_side, -16), jnp.where(lane >= 112, lanes(h_side, 16), h_main))[own]

    def fresh_side(flow_plane, tend_plane, total, depth, trans):
        safe = jnp.maximum(depth, 1.0)
        step = UV[flow_plane, BAND, :] + STEP * TEND[tend_plane, ALL, :]
        return jnp.where(depth > level, step + (trans - total) / safe, 0.0)

    def total_of(trans0, push):
        return trans0 + STEP * push

    u_sw = fresh_side(U_SW, U_SW, total_of(tx0_sw, push_x_sw), wx_sw, spread(tx_side, 0))
    u_se = fresh_side(U_SE, U_SE, total_of(tx0_se, push_x_se), wx_se, spread(tx_side, 96))
    v_sw = fresh_side(V_SW, V_SW, total_of(ty0_sw, push_y_sw), wy_sw, spread(ty_side, 0))
    v_se = fresh_side(V_SE, V_SE, total_of(ty0_se, push_y_se), wy_se, spread(ty_side, 96))

    gain_x = (tx_main - total_of(tx0, push_x)) / jnp.maximum(wx_main, 1.0)
    gain_y = (ty_main - total_of(ty0, push_y)) / jnp.maximum(wy_main, 1.0)
    for k in range(LEVELS):
        fresh = jnp.where(wx_main > k, UV[U_MAIN + k, BAND, :] + STEP * TEND[U_MAIN + k, ALL, :] + gain_x, 0.0)
        fresh = jnp.where(lane < 12, lanes(u_sw, -(32 * k + 16)), jnp.where(lane >= 116, lanes(u_se, 112 - 32 * k), fresh))
        NU[k] = fresh[own]
        u_out[k] = fresh[own]
        fresh = jnp.where(wy_main > k, UV[V_MAIN + k, BAND, :] + STEP * TEND[V_MAIN + k, ALL, :] + gain_y, 0.0)
        fresh = jnp.where(lane < 12, lanes(v_sw, -(32 * k + 16)), jnp.where(lane >= 116, lanes(v_se, 112 - 32 * k), fresh))
        NV[k] = fresh
        v_out[k] = fresh[own]

    ring_t = ring([TS[k, OWN, :] for k in range(LEVELS)])
    ring_s = ring([TS[4 + k, OWN, :] for k in range(LEVELS)])

    def side_flux(cells, flow):
        flux = flow * upwind_value(flow, *x_parts(cells))
        return flux - lanes(flux, 1)

    XS[0] = side_flux(jnp.where(half32, RTW[...], ring_t), u_sw[own])
    XS[1] = side_flux(jnp.where(half32, ring_t, lanes(RTE[...], 16)), u_se[own])
    XS[2] = side_flux(jnp.where(half32, lanes(RTW[...], -16), ring_s), u_sw[own])
    XS[3] = side_flux(jnp.where(half32, ring_s, RTE[...]), u_se[own])

    for field in range(2):
        out = (t_out, s_out)[field]
        for k in range(LEVELS):
            p = 4 * field + k
            flow = NU[k]
            flux = flow * jnp.where(flow >= 0.0, XU[p], XD[p])
            div_x = flux - lanes(flux, 1)
            div_x = jnp.where(lane32 < 8, lanes(XS[2 * field], -(32 * k + 16)),
                              jnp.where(lane32 >= 120, lanes(XS[2 * field + 1], 112 - 32 * k), div_x))
            up = NV[k, pl.ds(8, ROWS), :]
            down = NV[k, pl.ds(7, ROWS), :]
            flux_up = up * jnp.where(up >= 0.0, YU[p, pl.ds(1, ROWS), :], YD[p, pl.ds(1, ROWS), :])
            flux_down = down * jnp.where(down >= 0.0, YU[p, pl.ds(0, ROWS), :], YD[p, pl.ds(0, ROWS), :])
            cells = TS[p, OWN, :]
            fresh = cells - STEP * (div_x + (flux_up - flux_down))
            out[k] = jnp.where(wet[0] > k, fresh, 0.0)

    corner_n.wait_send()
    corner_s.wait_send()
    for copy in bulk + sides + relays:
        copy.wait_send()


def solution(mesh):
    n_lat, n_lon = mesh.shape["lat"], mesh.shape["lon"]

    def step(u_vel, v_vel, temp, salt, eta, wet_levels):
        levels = jax.ShapeDtypeStruct((LEVELS, ROWS, COLS), F32)
        plane = jax.ShapeDtypeStruct((ROWS, COLS), F32)
        hbm = pl.BlockSpec(memory_space=pl.ANY)
        vmem = pl.BlockSpec(memory_space=pltpu.VMEM)

        def body(*refs):
            kernel(n_lat, n_lon, *refs)

        return pl.pallas_call(
            body,
            out_shape=(levels, levels, levels, levels, plane),
            in_specs=[hbm] * 6,
            out_specs=(vmem,) * 5,
            scratch_shapes=[
                pltpu.VMEM((16, ROWS, COLS), F32),
                pltpu.VMEM((ROWS, COLS), F32),
                pltpu.VMEM((3, ROWS, COLS), jnp.int32),
                pltpu.VMEM((12, EXT, COLS), F32),
                pltpu.VMEM((8, EXT, COLS), F32),
                pltpu.VMEM((2, EXT, COLS), F32),
                pltpu.VMEM((3, EXT, COLS), F32),
                pltpu.VMEM((ROWS, COLS), F32),
                pltpu.VMEM((ROWS, COLS), F32),
                pltpu.VMEM((2, EXT, COLS), F32),
                pltpu.VMEM((2, EXT, COLS), F32),
                pltpu.VMEM((ROWS, COLS), F32),
                pltpu.VMEM((ROWS, COLS), F32),
                pltpu.VMEM((12, SPAN, COLS), F32),
                pltpu.VMEM((SPAN + 8, COLS), F32),
                pltpu.VMEM((8, ROWS, COLS), F32),
                pltpu.VMEM((8, ROWS, COLS), F32),
                pltpu.VMEM((8, 40, COLS), F32),
                pltpu.VMEM((8, 40, COLS), F32),
                pltpu.VMEM((4, SPAN, COLS), F32),
                pltpu.VMEM((4, ROWS, COLS), F32),
                pltpu.VMEM((4, ROWS, COLS), F32),
                pltpu.SemaphoreType.DMA((6,)),
                pltpu.SemaphoreType.DMA((16,)),
                pltpu.SemaphoreType.DMA((16,)),
            ],
            compiler_params=pltpu.CompilerParams(collective_id=0, has_side_effects=True),
        )(u_vel, v_vel, temp, salt, eta, wet_levels)

    tile, flat = P(None, "lat", "lon"), P("lat", "lon")
    return jax.shard_map(
        step, mesh=mesh, in_specs=(tile, tile, tile, tile, flat, tile),
        out_specs=(tile, tile, tile, tile, flat), check_vma=False)
```

time: 380 us -> 50.8 us (0.13)
  the two profiles are of different devices: /device:TPU:25 before, /device:TPU:6 now
where the time goes in v1:
time: 50.8 us; the launch traced here: 50.4 us
  Pallas kernels  45.2 us (89%)
  local copies, waits for them, and re-layouts  4.55 us (9%)
  between operations  0.65 us (1%)
    pallas_call x1, Pallas kernels, step(): pl.pallas_call(body, out_shape=(levels, levels, levels, levels, plane), i...  45.2 us
    unnamed x13, local copies, waits for them, and re-layouts  4.55 us

profile of v1, /device:TPU:6, one launch (start us, length us, event | category | flops | bytes accessed | tf_op | source)
XLA Modules:
  0.0 50.4 jit_solution(6343082571265080985)
XLA Ops:
  0.6 45.2 %shard_map.101 = (f32[4,32,128]{2,1,0:T(8,128)}, f32[4,32,128]{2,1,0:T(8,128)}, f32[4,32,128]{2,1,0:T(8,128)}, f32[4,32,128]{2,1,0:T(8,128)}, f32[32,128]{1,0:T(8,128)}) custom-call(f32[4,32,128]{2,1,0:T(8,128)} %refs_0_.1, f32[4,32,128]{2,1,0:T(8,128)} %refs_1_.1, f32[4,32,128]{2,1,0:T(8,128)} %refs_2_.1, f32[4,32,128]{2,1,0:T(8,128)} %refs_3_.1, ...), custom_call_target="tpu_custom_call" | custom-call | tf_op jit(solution)/shard_map/pallas_call | solution.py:423
  45.8 0.0 copy-start.2
  45.8 1.5 %copy.16 = f32[4,32,128]{2,1,0:T(8,128)} copy(f32[4,32,128]{2,1,0:T(8,128)} %get-tuple-element.10) | data formatting | bytes 131072
  47.3 0.0 copy-done.2
  47.3 0.0 copy-start.1
  47.3 0.6 %copy.17 = f32[4,32,128]{2,1,0:T(8,128)} copy(f32[4,32,128]{2,1,0:T(8,128)S(1)} %copy-done.2) | data formatting | bytes 131072
  48.0 0.2 copy-done.1
  48.2 0.0 copy-start
  48.2 0.6 %copy.18 = f32[4,32,128]{2,1,0:T(8,128)} copy(f32[4,32,128]{2,1,0:T(8,128)S(1)} %copy-done.1) | data formatting | bytes 131072
  48.8 0.2 copy-done
  49.0 0.0 copy-start.3
  49.1 0.6 %copy.19 = f32[4,32,128]{2,1,0:T(8,128)} copy(f32[4,32,128]{2,1,0:T(8,128)S(1)} %copy-done) | data formatting | bytes 131072
  49.7 0.1 copy-done.3
  49.8 0.6 %copy.20 = f32[32,128]{1,0:T(8,128)} copy(f32[32,128]{1,0:T(8,128)S(1)} %copy-done.3) | data formatting | bytes 32768
Async XLA Ops:
  45.8 1.5 %copy-start.2 = (f32[4,32,128]{2,1,0:T(8,128)S(1)}, f32[4,32,128]{2,1,0:T(8,128)}, u32[]{:S(2)}) copy-start(f32[4,32,128]{2,1,0:T(8,128)} %get-tuple-element.11) | copy-start | bytes 196612
  47.3 0.9 %copy-start.1 = (f32[4,32,128]{2,1,0:T(8,128)S(1)}, f32[4,32,128]{2,1,0:T(8,128)}, u32[]{:S(2)}) copy-start(f32[4,32,128]{2,1,0:T(8,128)} %get-tuple-element.12) | copy-start | bytes 196612
  48.2 0.9 %copy-start = (f32[4,32,128]{2,1,0:T(8,128)S(1)}, f32[4,32,128]{2,1,0:T(8,128)}, u32[]{:S(2)}) copy-start(f32[4,32,128]{2,1,0:T(8,128)} %get-tuple-element.13) | copy-start | bytes 196612
  49.0 0.7 %copy-start.3 = (f32[32,128]{1,0:T(8,128)S(1)}, f32[32,128]{1,0:T(8,128)}, u32[]{:S(2)}) copy-start(f32[32,128]{1,0:T(8,128)} %get-tuple-element.14) | copy-start | bytes 49156

commit v2 on v1

--- a/solution.py
+++ b/solution.py
@@ -89,21 +89,33 @@
     return level_sum(jnp.where((lane >= start) & (lane < start + 32), x, 0.0))
 
 
+DIRS = ((1, 0), (-1, 0), (0, 1), (0, -1), (1, 1), (-1, 1), (1, -1), (-1, -1))
+NORTH, SOUTH, EAST, WEST, NE, SE, NW, SW = range(8)
+
+
 def kernel(n_lat, n_lon, u_hbm, v_hbm, t_hbm, s_hbm, e_hbm, w_hbm,
-           u_out, v_out, t_out, s_out, e_out,
-           raw, raw2, wet, UV, TS, WE, PK, TE, TW, RW, RE, RTW, RTE,
+           result,
+           raw, raw2, wet, UV, TS, WE, PE, PW, RW, RE,
            TEND, FY, XU, XD, YU, YD, NV, NU, XS,
-           in_sem, send_sem, recv_sem):
+           in_sem, ready, send_sem, recv_sem):
     lat = lax.axis_index("lat")
     lon = lax.axis_index("lon")
-    north = (lax.rem(lat + 1, n_lat), lon)
-    south = (lax.rem(lat + n_lat - 1, n_lat), lon)
-    east = (lat, lax.rem(lon + 1, n_lon))
-    west = (lat, lax.rem(lon + n_lon - 1, n_lon))
+
+    def start_rank(i, j):
+        return ((j // 8) * 8 + lax.rem(i, 8)) * (n_lat * n_lon) + i * n_lon + j
+
+    peers = [(lax.rem(lat + n_lat + di, n_lat), lax.rem(lon + n_lon + dj, n_lon)) for di, dj in DIRS]
+    here = start_rank(lat, lon)
+    earlier = [start_rank(*peer) < here for peer in peers]
 
     barrier = pltpu.get_barrier_semaphore()
-    for peer in (north, south, east, west):
-        pl.semaphore_signal(barrier, inc=1, device_id=peer, device_id_type=MESH)
+    expected = 0
+    for d in range(8):
+        expected = expected + jnp.where(earlier[d], 1, 0)
+
+        @pl.when(jnp.logical_not(earlier[d]))
+        def _():
+            pl.semaphore_signal(barrier, inc=1, device_id=peers[d], device_id_type=MESH)
 
     loads = [
         pltpu.make_async_copy(w_hbm, wet, in_sem.at[0]),
@@ -131,52 +143,72 @@
     half32 = lax.rem(lane32, 32) < 16
     ring_u = ring([UV[U_MAIN + k, OWN, :] for k in range(LEVELS)])
     ring_v = ring([UV[V_MAIN + k, OWN, :] for k in range(LEVELS)])
-    PK[0, OWN, :] = jnp.where(half32, ring_u, lanes(ring_v, 16))
-    PK[1, OWN, :] = jnp.where(lane32 < 32, lanes(raw2[...], 16), lanes(wet[0].astype(F32), 48))
-    PK[2, OWN, :] = jnp.where(half32, lanes(ring_u, -16), ring_v)
     ring_t = ring([TS[k, OWN, :] for k in range(LEVELS)])
     ring_s = ring([TS[4 + k, OWN, :] for k in range(LEVELS)])
-    TE[...] = jnp.where(half32, ring_t, lanes(ring_s, 16))
-    TW[...] = jnp.where(half32, lanes(ring_t, -16), ring_s)
-
-    pl.semaphore_wait(barrier, 4)
-
-    def send(slot, src, dst, peer):
-        copy = pltpu.make_async_remote_copy(
-            src_ref=src, dst_ref=dst, send_sem=send_sem.at[slot], recv_sem=recv_sem.at[slot],
-            device_id=peer, device_id_type=MESH)
-        copy.start()
-        return copy
+    eta8, wet24 = lanes(raw2[...], 8), lanes(wet[0].astype(F32), 24)
+    PE[0, OWN, :] = jnp.where(half32, ring_u, lanes(ring_v, 16))
+    PW[0, OWN, :] = jnp.where(half32, lanes(ring_u, -16), ring_v)
+    PE[1, OWN, :] = jnp.where(lane32 < 8, eta8, jnp.where(
+        (lane32 >= 16) & (lane32 < 24), wet24, jnp.where(half32, ring_t, lanes(ring_s, 16))))
+    PW[1, OWN, :] = jnp.where((lane32 >= 8) & (lane32 < 16), eta8, jnp.where(
+        (lane32 >= 24) & (lane32 < 32), wet24, jnp.where(half32, lanes(ring_t, -16), ring_s)))
 
     top, bottom = pl.ds(32, 16), pl.ds(16, 16)
     under, over = pl.ds(0, 16), pl.ds(48, 16)
     every = pl.ds(0, 8)
-    corner_n = send(0, PK.at[:, top, :], PK.at[:, under, :], north)
-    corner_s = send(1, PK.at[:, bottom, :], PK.at[:, over, :], south)
-    bulk = [
-        send(2, UV.at[every, top, :], UV.at[every, under, :], north),
-        send(3, UV.at[every, bottom, :], UV.at[every, over, :], south),
-        send(4, WE.at[:, top, :], WE.at[:, under, :], north),
-        send(5, WE.at[:, bottom, :], WE.at[:, over, :], south),
-        send(6, TS.at[:, pl.ds(40, 8), :], TS.at[:, pl.ds(8, 8), :], north),
-        send(7, TS.at[:, pl.ds(16, 8), :], TS.at[:, pl.ds(48, 8), :], south),
-    ]
-    sides = [
-        send(8, PK.at[pl.ds(0, 2), OWN, :], RW.at[:, OWN, :], east),
-        send(9, PK.at[pl.ds(1, 2), OWN, :], RE.at[:, OWN, :], west),
-        send(10, TE, RTW, east),
-        send(11, TW, RTE, west),
-    ]
-    corner_n.wait_recv()
-    relays = [
-        send(12, PK.at[pl.ds(0, 2), under, :], RW.at[:, under, :], east),
-        send(13, PK.at[pl.ds(1, 2), under, :], RE.at[:, under, :], west),
-    ]
-    corner_s.wait_recv()
-    relays += [
-        send(14, PK.at[pl.ds(0, 2), over, :], RW.at[:, over, :], east),
-        send(15, PK.at[pl.ds(1, 2), over, :], RE.at[:, over, :], west),
-    ]
+    parcels = {
+        NORTH: [(UV.at[every, top, :], UV.at[every, under, :]),
+                (WE.at[:, top, :], WE.at[:, under, :]),
+                (TS.at[:, pl.ds(40, 8), :], TS.at[:, pl.ds(8, 8), :])],
+        SOUTH: [(UV.at[every, bottom, :], UV.at[every, over, :]),
+                (WE.at[:, bottom, :], WE.at[:, over, :]),
+                (TS.at[:, pl.ds(16, 8), :], TS.at[:, pl.ds(48, 8), :])],
+        EAST: [(PE.at[:, OWN, :], RW.at[:, OWN, :])],
+        WEST: [(PW.at[:, OWN, :], RE.at[:, OWN, :])],
+        NE: [(PE.at[:, top, :], RW.at[:, under, :])],
+        SE: [(PE.at[:, bottom, :], RW.at[:, over, :])],
+        NW: [(PW.at[:, top, :], RE.at[:, under, :])],
+        SW: [(PW.at[:, bottom, :], RE.at[:, over, :])],
+    }
+    first_slot, slots = {}, 0
+    for d in range(8):
+        first_slot[d] = slots
+        slots += len(parcels[d])
+
+    def copies(d):
+        return [
+            pltpu.make_async_remote_copy(
+                src_ref=src, dst_ref=dst, send_sem=send_sem.at[first_slot[d] + i], recv_sem=recv_sem.at[first_slot[d] + i],
+                device_id=peers[d], device_id_type=MESH)
+            for i, (src, dst) in enumerate(parcels[d])]
+
+    def send_to_earlier(d):
+        @pl.when(earlier[d])
+        def _():
+            for copy in copies(d):
+                copy.start()
+
+    def send_to_later(d):
+        @pl.when(jnp.logical_not(earlier[d]))
+        def _():
+            pl.semaphore_wait(ready.at[d], 1)
+            for copy in copies(d):
+                copy.start()
+
+    def wait_from(d):
+        for copy in copies(d):
+            copy.wait_recv()
+
+    @pl.when(expected > 0)
+    def _():
+        pl.semaphore_wait(barrier, expected)
+
+    for d in (EAST, NE, SE, WEST, NW, SW):
+        send_to_earlier(d)
+    for d in range(8):
+        @pl.when(earlier[d])
+        def _():
+            pl.semaphore_signal(ready.at[DIRS.index((-DIRS[d][0], -DIRS[d][1]))], inc=1, device_id=peers[d], device_id_type=MESH)
 
     def tracer_x(k, carry):
         for r0 in range(0, ROWS, 16):
@@ -187,8 +219,12 @@
 
     lax.fori_loop(0, 8, tracer_x, 0)
 
-    for copy in bulk:
-        copy.wait_recv()
+    for d in (NORTH, SOUTH):
+        send_to_earlier(d)
+    for d in (NORTH, SOUTH, EAST, NE, SE):
+        send_to_later(d)
+    for d in (NORTH, SOUTH):
+        wait_from(d)
 
     zero16 = jnp.zeros((16, COLS), F32)
     FY[pl.ds(SPAN, 8), :] = jnp.zeros((8, COLS), F32)
@@ -236,8 +272,10 @@
 
     lax.fori_loop(0, 8, tracer_y, 0)
 
-    for copy in sides + relays:
-        copy.wait_recv()
+    for d in (WEST, NW, SW):
+        send_to_later(d)
+    for d in (EAST, WEST, NE, SE, NW, SW):
+        wait_from(d)
 
     @pl.when(lat == 0)
     def _():
@@ -257,8 +295,8 @@
     ring_v = ring([UV[V_MAIN + k] for k in range(LEVELS)])
     UV[U_SW] = jnp.where(half, RW[0], ring_u)
     UV[V_SW] = jnp.where(half, lanes(RW[0], -16), ring_v)
-    UV[U_SE] = jnp.where(half, ring_u, lanes(RE[1], 16))
-    UV[V_SE] = jnp.where(half, ring_v, RE[1])
+    UV[U_SE] = jnp.where(half, ring_u, lanes(RE[0], 16))
+    UV[V_SE] = jnp.where(half, ring_v, RE[0])
 
     def strips(i, carry):
         tendency(U_SW + i, U_SW + i, V_SW + i, U_SW + i)
@@ -267,9 +305,6 @@
 
     lax.fori_loop(0, 2, strips, 0)
 
-    own_2d = jnp.where(lane64 < 32, lanes(WE[1], 16), lanes(WE[0], 48))
-    west_2d = jnp.where(half, RW[1], own_2d)
-    east_2d = jnp.where(half, own_2d, RE[0])
     lane = lax.broadcasted_iota(jnp.int32, (SPAN, COLS), 1)
     level = (lane // 32).astype(F32)
     BAND = pl.ds(LO, SPAN)
@@ -283,11 +318,14 @@
     def shifted_up(x):
         return rows(x, -1)
 
-    wet_sw = spread(west_2d, 32)
-    wet_se = spread(east_2d, 32)
     wet_main = WE[0]
+    wet_own = lanes(wet_main, 16)
+    wet_sw = spread(jnp.where(lane64 < 16, lanes(RW[1], -8), wet_own), 0)
+    wet_se = spread(jnp.where(lane64 < 16, wet_own, lanes(RE[1], -8)), 0)
     eta_main = WE[1, BAND, :]
-    eta_side = joined(spread(band(west_2d), 0), eta_main, spread(band(east_2d), 0))
+    eta_own = lanes(eta_main, 16)
+    eta_side = joined(spread(jnp.where(lane < 16, lanes(RW[1, BAND, :], 8), eta_own), 0), eta_main,
+                      spread(jnp.where(lane < 16, eta_own, lanes(RE[1, BAND, :], 8)), 0))
 
     def faces(w):
         here = band(w)
@@ -346,7 +384,7 @@
         WAVE * wx_side, WAVE * wy_side)
 
     own = slice(PAD - LO, PAD - LO + ROWS)
-    e_out[...] = jnp.where(lane < 16, lanes(h_side, -16), jnp.where(lane >= 112, lanes(h_side, 16), h_main))[own]
+    result[16] = jnp.where(lane < 16, lanes(h_side, -16), jnp.where(lane >= 112, lanes(h_side, 16), h_main))[own]
 
     def fresh_side(flow_plane, tend_plane, total, depth, trans):
         safe = jnp.maximum(depth, 1.0)
@@ -367,11 +405,11 @@
         fresh = jnp.where(wx_main > k, UV[U_MAIN + k, BAND, :] + STEP * TEND[U_MAIN + k, ALL, :] + gain_x, 0.0)
         fresh = jnp.where(lane < 12, lanes(u_sw, -(32 * k + 16)), jnp.where(lane >= 116, lanes(u_se, 112 - 32 * k), fresh))
         NU[k] = fresh[own]
-        u_out[k] = fresh[own]
+        result[k] = fresh[own]
         fresh = jnp.where(wy_main > k, UV[V_MAIN + k, BAND, :] + STEP * TEND[V_MAIN + k, ALL, :] + gain_y, 0.0)
         fresh = jnp.where(lane < 12, lanes(v_sw, -(32 * k + 16)), jnp.where(lane >= 116, lanes(v_se, 112 - 32 * k), fresh))
         NV[k] = fresh
-        v_out[k] = fresh[own]
+        result[4 + k] = fresh[own]
 
     ring_t = ring([TS[k, OWN, :] for k in range(LEVELS)])
     ring_s = ring([TS[4 + k, OWN, :] for k in range(LEVELS)])
@@ -380,13 +418,12 @@
         flux = flow * upwind_value(flow, *x_parts(cells))
         return flux - lanes(flux, 1)
 
-    XS[0] = side_flux(jnp.where(half32, RTW[...], ring_t), u_sw[own])
-    XS[1] = side_flux(jnp.where(half32, ring_t, lanes(RTE[...], 16)), u_se[own])
-    XS[2] = side_flux(jnp.where(half32, lanes(RTW[...], -16), ring_s), u_sw[own])
-    XS[3] = side_flux(jnp.where(half32, ring_s, RTE[...]), u_se[own])
+    XS[0] = side_flux(jnp.where(half32, RW[1, OWN, :], ring_t), u_sw[own])
+    XS[1] = side_flux(jnp.where(half32, ring_t, lanes(RE[1, OWN, :], 16)), u_se[own])
+    XS[2] = side_flux(jnp.where(half32, lanes(RW[1, OWN, :], -16), ring_s), u_sw[own])
+    XS[3] = side_flux(jnp.where(half32, ring_s, RE[1, OWN, :]), u_se[own])
 
     for field in range(2):
-        out = (t_out, s_out)[field]
         for k in range(LEVELS):
             p = 4 * field + k
             flow = NU[k]
@@ -400,12 +437,18 @@
             flux_down = down * jnp.where(down >= 0.0, YU[p, pl.ds(0, ROWS), :], YD[p, pl.ds(0, ROWS), :])
             cells = TS[p, OWN, :]
             fresh = cells - STEP * (div_x + (flux_up - flux_down))
-            out[k] = jnp.where(wet[0] > k, fresh, 0.0)
-
-    corner_n.wait_send()
-    corner_s.wait_send()
-    for copy in bulk + sides + relays:
-        copy.wait_send()
+            result[8 + p] = jnp.where(wet[0] > k, fresh, 0.0)
+
+    for d in range(8):
+        for copy in copies(d):
+            copy.wait_send()
+
+
+def deal(result, u_out, v_out, t_out, s_out, e_out):
+    for i, out in enumerate((u_out, v_out, t_out, s_out)):
+        for k in range(LEVELS):
+            out[k] = result[LEVELS * i + k]
+    e_out[...] = result[16]
 
 
 def solution(mesh):
@@ -420,40 +463,47 @@
         def body(*refs):
             kernel(n_lat, n_lon, *refs)
 
-        return pl.pallas_call(
+        def buffer(*shape):
+            return pltpu.VMEM(shape, F32)
+
+        result = pl.pallas_call(
             body,
-            out_shape=(levels, levels, levels, levels, plane),
+            out_shape=jax.ShapeDtypeStruct((17, ROWS, COLS), F32),
             in_specs=[hbm] * 6,
-            out_specs=(vmem,) * 5,
+            out_specs=vmem,
             scratch_shapes=[
-                pltpu.VMEM((16, ROWS, COLS), F32),
-                pltpu.VMEM((ROWS, COLS), F32),
+                buffer(16, ROWS, COLS),
+                buffer(ROWS, COLS),
                 pltpu.VMEM((3, ROWS, COLS), jnp.int32),
-                pltpu.VMEM((12, EXT, COLS), F32),
-                pltpu.VMEM((8, EXT, COLS), F32),
-                pltpu.VMEM((2, EXT, COLS), F32),
-                pltpu.VMEM((3, EXT, COLS), F32),
-                pltpu.VMEM((ROWS, COLS), F32),
-                pltpu.VMEM((ROWS, COLS), F32),
-                pltpu.VMEM((2, EXT, COLS), F32),
-                pltpu.VMEM((2, EXT, COLS), F32),
-                pltpu.VMEM((ROWS, COLS), F32),
-                pltpu.VMEM((ROWS, COLS), F32),
-                pltpu.VMEM((12, SPAN, COLS), F32),
-                pltpu.VMEM((SPAN + 8, COLS), F32),
-                pltpu.VMEM((8, ROWS, COLS), F32),
-                pltpu.VMEM((8, ROWS, COLS), F32),
-                pltpu.VMEM((8, 40, COLS), F32),
-                pltpu.VMEM((8, 40, COLS), F32),
-                pltpu.VMEM((4, SPAN, COLS), F32),
-                pltpu.VMEM((4, ROWS, COLS), F32),
-                pltpu.VMEM((4, ROWS, COLS), F32),
+                buffer(12, EXT, COLS),
+                buffer(8, EXT, COLS),
+                buffer(2, EXT, COLS),
+                buffer(2, EXT, COLS),
+                buffer(2, EXT, COLS),
+                buffer(2, EXT, COLS),
+                buffer(2, EXT, COLS),
+                buffer(12, SPAN, COLS),
+                buffer(SPAN + 8, COLS),
+                buffer(8, ROWS, COLS),
+                buffer(8, ROWS, COLS),
+                buffer(8, 40, COLS),
+                buffer(8, 40, COLS),
+                buffer(4, SPAN, COLS),
+                buffer(4, ROWS, COLS),
+                buffer(4, ROWS, COLS),
                 pltpu.SemaphoreType.DMA((6,)),
-                pltpu.SemaphoreType.DMA((16,)),
-                pltpu.SemaphoreType.DMA((16,)),
+                pltpu.SemaphoreType.REGULAR((8,)),
+                pltpu.SemaphoreType.DMA((12,)),
+                pltpu.SemaphoreType.DMA((12,)),
             ],
             compiler_params=pltpu.CompilerParams(collective_id=0, has_side_effects=True),
         )(u_vel, v_vel, temp, salt, eta, wet_levels)
+        return pl.pallas_call(
+            deal,
+            out_shape=(levels, levels, levels, levels, plane),
+            in_specs=[vmem],
+            out_specs=(vmem,) * 5,
+        )(result)
 
     tile, flat = P(None, "lat", "lon"), P("lat", "lon")
     return jax.shard_map(

time: 50.8 us -> 44.1 us (0.87)
  the two profiles are of different devices: /device:TPU:6 before, /device:TPU:998 now
where the time goes in v2:
time: 44.1 us; the launch traced here: 43.9 us
  Pallas kernels  43.3 us (98%)
  between operations  0.64 us (1%)
    pallas_call x1, Pallas kernels, step(): pl.pallas_call(body, out_shape=jax.ShapeDtypeStruct((17, ROWS, COLS), F32...  41.6 us
    pallas_call x1, Pallas kernels, step(): pl.pallas_call(deal, out_shape=(levels, levels, levels, levels, plane), i...  1.66 us

profile of v2, /device:TPU:998, one launch (start us, length us, event | category | flops | bytes accessed | tf_op | source)
XLA Modules:
  0.0 43.9 jit_solution(7254796801091481212)
XLA Ops:
  0.6 41.6 %shard_map.101.result = f32[17,32,128]{2,1,0:T(8,128)} custom-call(f32[4,32,128]{2,1,0:T(8,128)} %refs_0_.1, f32[4,32,128]{2,1,0:T(8,128)} %refs_1_.1, f32[4,32,128]{2,1,0:T(8,128)} %refs_2_.1, f32[4,32,128]{2,1,0:T(8,128)} %refs_3_.1, f32[32,128]{1,0:T(8,128)} %refs_4_.1, s32[3,32,128]{2,1,0:T(8,128)} %refs_5_.1), custom_call_target="tpu_custom_call" | custom-call | tf_op jit(solution)/shard_map/pallas_call | solution.py:469
  42.3 1.7 %shard_map.102 = (f32[4,32,128]{2,1,0:T(8,128)}, f32[4,32,128]{2,1,0:T(8,128)}, f32[4,32,128]{2,1,0:T(8,128)}, f32[4,32,128]{2,1,0:T(8,128)}, f32[32,128]{1,0:T(8,128)}) custom-call(f32[17,32,128]{2,1,0:T(8,128)} %shard_map.101.result), custom_call_target="tpu_custom_call" | custom-call | tf_op jit(solution)/shard_map/pallas_call | solution.py:501

commit v3 on v2

v3 whole, which is shorter than its diff:
```python
import jax
import jax.numpy as jnp
from jax import lax
from jax.experimental import pallas as pl
from jax.experimental.pallas import tpu as pltpu
from jax.sharding import PartitionSpec as P

MESH = pl.DeviceIdType.MESH
F32 = jnp.float32
LEVELS = 4
SUB = 8
BLOCK = 8
STEP = 0.4
WAVE = 0.45 / 4
EPS = 1e-6 * 12.0 / 13.0
ROWS = 32
COLS = 128
PAD = 16
EXT = ROWS + 2 * PAD
LO = 8
SPAN = 48

U_MAIN, V_MAIN, U_SW, U_SE, V_SW, V_SE = 0, 4, 8, 9, 10, 11


def lanes(x, shift):
    shift = shift % COLS
    return x if shift == 0 else pltpu.roll(x, shift, 1)


def rows(x, shift):
    return pltpu.roll(x, shift % x.shape[0], 0)


def correction(d0, d1, d2, d3):
    x0 = d1 - d0
    x1 = d2 - d1
    x2 = d3 - d2
    m1 = d1 + d1
    m2 = d2 + d2
    y0 = x0 + m1
    y1 = d1 + d2
    y2 = x2 - m2
    e0 = x0 * x0 + (y0 * y0) * (3.0 / 13.0) + EPS
    e1 = x1 * x1 + (y1 * y1) * (3.0 / 13.0) + EPS
    e2 = x2 * x2 + (y2 * y2) * (3.0 / 13.0) + EPS
    a0 = e1 * e2
    a1 = e0 * e2
    a2 = e0 * e1
    w0 = a0 * a0
    w1 = (a1 * a1) * 6.0
    w2 = (a2 * a2) * 3.0
    top = w0 * (5.0 * d1 - 2.0 * d0) + w1 * (d1 + m2) + w2 * (4.0 * d2 - d3)
    return top / ((w0 + w1 + w2) * 6.0)


def upwind_value(flow, q0, q1, gm2, gm1, g0, g1, g2):
    ahead = flow >= 0.0
    fix = correction(jnp.where(ahead, gm2, g2), jnp.where(ahead, gm1, g1), g0, jnp.where(ahead, g1, gm1))
    return jnp.where(ahead, q0 + fix, q1 - fix)


def x_parts(q):
    q1 = lanes(q, -1)
    g = q1 - q
    return q, q1, lanes(g, 2), lanes(g, 1), g, lanes(g, -1), lanes(g, -2)


def y_parts(ref, k, r0, n):
    q = [ref[k, pl.ds(r0 + s, n), :] for s in range(-2, 4)]
    g = [q[i + 1] - q[i] for i in range(5)]
    return q[2], q[3], g[0], g[1], g[2], g[3], g[4]


def ring(parts):
    lane = lax.broadcasted_iota(jnp.int32, parts[0].shape, 1)
    out = lanes(parts[0], 16)
    for k in range(1, LEVELS):
        out = jnp.where(lane >= 32 * k, lanes(parts[k], 32 * k + 16), out)
    return out


def level_sum(x):
    y = x + lanes(x, 64)
    return y + lanes(y, 32)


def spread(x, start):
    lane = lax.broadcasted_iota(jnp.int32, x.shape, 1)
    return level_sum(jnp.where((lane >= start) & (lane < start + 32), x, 0.0))


DIRS = ((1, 0), (-1, 0), (0, 1), (0, -1), (1, 1), (-1, 1), (1, -1), (-1, -1))
NORTH, SOUTH, EAST, WEST, NE, SE, NW, SW = range(8)


def kernel(n_lat, n_lon, u_hbm, v_hbm, t_hbm, s_hbm, e_hbm, w_hbm,
           result,
           raw, raw2, wet, UV, TS, WE, PE, PW, RW, RE, HUB, KEPT,
           TEND, FY, XU, XD, YU, YD, NV, NU, XS,
           in_sem, ready, send_sem, recv_sem):
    lat = lax.axis_index("lat")
    lon = lax.axis_index("lon")

    def start_rank(i, j):
        group = j // BLOCK
        group = jnp.where(group == 2, 3, jnp.where(group == 3, 2, group))
        return (group * BLOCK + lax.rem(i, BLOCK)) * (n_lat * n_lon) + i * n_lon + j

    peers = [(lax.rem(lat + n_lat + di, n_lat), lax.rem(lon + n_lon + dj, n_lon)) for di, dj in DIRS]
    here = start_rank(lat, lon)
    earlier = [start_rank(*peer) < here for peer in peers]
    first_row, last_row = lax.rem(lat, BLOCK) == 0, lax.rem(lat, BLOCK) == BLOCK - 1
    first_column, last_column = lax.rem(lon, BLOCK) == 0, lax.rem(lon, BLOCK) == BLOCK - 1
    far_a = first_row & last_column
    far_b = last_row & first_column
    hub = first_row & first_column
    later = [jnp.logical_not(flag) for flag in earlier]
    for d, far in ((SE, far_a), (NW, far_b)):
        earlier[d] = earlier[d] & jnp.logical_not(far)
        later[d] = later[d] & jnp.logical_not(far)

    barrier = pltpu.get_barrier_semaphore()
    expected = 0
    for d in range(8):
        expected = expected + jnp.where(earlier[d], 1, 0)

        @pl.when(later[d])
        def _():
            pl.semaphore_signal(barrier, inc=1, device_id=peers[d], device_id_type=MESH)

    loads = [
        pltpu.make_async_copy(w_hbm, wet, in_sem.at[0]),
        pltpu.make_async_copy(u_hbm, raw.at[pl.ds(0, 4)], in_sem.at[1]),
        pltpu.make_async_copy(v_hbm, raw.at[pl.ds(4, 4)], in_sem.at[2]),
        pltpu.make_async_copy(t_hbm, raw.at[pl.ds(8, 4)], in_sem.at[3]),
        pltpu.make_async_copy(s_hbm, raw.at[pl.ds(12, 4)], in_sem.at[4]),
        pltpu.make_async_copy(e_hbm, raw2, in_sem.at[5]),
    ]
    for load in loads:
        load.start()
    for load in loads:
        load.wait()

    OWN = pl.ds(PAD, ROWS)
    for k in range(LEVELS):
        UV[U_MAIN + k, OWN, :] = jnp.where(wet[1] > k, raw[k], 0.0)
        UV[V_MAIN + k, OWN, :] = jnp.where(wet[2] > k, raw[4 + k], 0.0)
        TS[k, OWN, :] = jnp.where(wet[0] > k, raw[8 + k], 0.0)
        TS[4 + k, OWN, :] = jnp.where(wet[0] > k, raw[12 + k], 0.0)
    WE[0, OWN, :] = wet[0].astype(F32)
    WE[1, OWN, :] = raw2[...]

    lane32 = lax.broadcasted_iota(jnp.int32, (ROWS, COLS), 1)
    half32 = lax.rem(lane32, 32) < 16
    ring_u = ring([UV[U_MAIN + k, OWN, :] for k in range(LEVELS)])
    ring_v = ring([UV[V_MAIN + k, OWN, :] for k in range(LEVELS)])
    ring_t = ring([TS[k, OWN, :] for k in range(LEVELS)])
    ring_s = ring([TS[4 + k, OWN, :] for k in range(LEVELS)])
    eta8, wet24 = lanes(raw2[...], 8), lanes(wet[0].astype(F32), 24)
    PE[0, OWN, :] = jnp.where(half32, ring_u, lanes(ring_v, 16))
    PW[0, OWN, :] = jnp.where(half32, lanes(ring_u, -16), ring_v)
    PE[1, OWN, :] = jnp.where(lane32 < 8, eta8, jnp.where(
        (lane32 >= 16) & (lane32 < 24), wet24, jnp.where(half32, ring_t, lanes(ring_s, 16))))
    PW[1, OWN, :] = jnp.where((lane32 >= 8) & (lane32 < 16), eta8, jnp.where(
        (lane32 >= 24) & (lane32 < 32), wet24, jnp.where(half32, lanes(ring_t, -16), ring_s)))

    top, bottom = pl.ds(32, 16), pl.ds(16, 16)
    under, over = pl.ds(0, 16), pl.ds(48, 16)
    every = pl.ds(0, 8)
    parcels = {
        NORTH: [(UV.at[every, pl.ds(36, 12), :], UV.at[every, pl.ds(4, 12), :]),
                (WE.at[:, pl.ds(40, 8), :], WE.at[:, pl.ds(8, 8), :]),
                (TS.at[:, pl.ds(45, 3), :], TS.at[:, pl.ds(13, 3), :])],
        SOUTH: [(UV.at[every, pl.ds(16, 12), :], UV.at[every, pl.ds(48, 12), :]),
                (WE.at[:, pl.ds(16, 8), :], WE.at[:, pl.ds(48, 8), :]),
                (TS.at[:, pl.ds(16, 3), :], TS.at[:, pl.ds(48, 3), :])],
        EAST: [(PE.at[:, OWN, :], RW.at[:, OWN, :])],
        WEST: [(PW.at[:, OWN, :], RE.at[:, OWN, :])],
        NE: [(PE.at[:, pl.ds(36, 12), :], RW.at[:, pl.ds(4, 12), :])],
        SE: [(PE.at[:, pl.ds(16, 12), :], RW.at[:, pl.ds(48, 12), :])],
        NW: [(PW.at[:, pl.ds(36, 12), :], RE.at[:, pl.ds(4, 12), :])],
        SW: [(PW.at[:, pl.ds(16, 12), :], RE.at[:, pl.ds(48, 12), :])],
    }
    first_slot, slots = {}, 0
    for d in range(8):
        first_slot[d] = slots
        slots += len(parcels[d])

    def copies(d):
        return [
            pltpu.make_async_remote_copy(
                src_ref=src, dst_ref=dst, send_sem=send_sem.at[first_slot[d] + i], recv_sem=recv_sem.at[first_slot[d] + i],
                device_id=peers[d], device_id_type=MESH)
            for i, (src, dst) in enumerate(parcels[d])]

    def send_to_earlier(d):
        @pl.when(earlier[d])
        def _():
            for copy in copies(d):
                copy.start()

    def send_to_later(d):
        @pl.when(later[d])
        def _():
            pl.semaphore_wait(ready.at[d], 1)
            for copy in copies(d):
                copy.start()

    def wait_from(d):
        for copy in copies(d):
            copy.wait_recv()

    def extra(slot, src, dst, arrival, peer):
        return pltpu.make_async_remote_copy(
            src_ref=src, dst_ref=dst, send_sem=send_sem.at[slot], recv_sem=recv_sem.at[arrival],
            device_id=peer, device_id_type=MESH)

    to_hub = extra(slots, PW.at[:, pl.ds(36, 12), :], HUB.at[:, pl.ds(4, 12), :], slots, peers[NORTH])
    hub_west = extra(slots + 1, HUB.at[:, pl.ds(4, 12), :], RE.at[:, pl.ds(4, 12), :], first_slot[NW], peers[WEST])
    hub_south = extra(slots + 2, RW.at[:, pl.ds(16, 12), :], RW.at[:, pl.ds(48, 12), :], first_slot[SE], peers[SOUTH])

    @pl.when(expected > 0)
    def _():
        pl.semaphore_wait(barrier, expected)

    for d in range(8):
        @pl.when(earlier[d])
        def _():
            pl.semaphore_signal(ready.at[DIRS.index((-DIRS[d][0], -DIRS[d][1]))], inc=1, device_id=peers[d], device_id_type=MESH)

    for d in (EAST, NE, SE, WEST, NW, SW, NORTH, SOUTH):
        send_to_earlier(d)

    @pl.when(far_b & earlier[NORTH])
    def _():
        to_hub.start()

    def flux_x(q_plane, u_plane, r0, n):
        flow = UV[u_plane, pl.ds(r0, n), :]
        flux = flow * upwind_value(flow, *x_parts(UV[q_plane, pl.ds(r0, n), :]))
        return flux - lanes(flux, 1)

    def flux_y(q_plane, v_plane, r0):
        flow = UV[v_plane, pl.ds(r0, 8), :]
        return flow * upwind_value(flow, *y_parts(UV, q_plane, r0, 8))

    def put_x(q_plane, u_plane, r0, n):
        TEND[q_plane, pl.ds(r0 - LO, n), :] = flux_x(q_plane, u_plane, r0, n)

    def put_y(q_plane, v_plane, r0):
        FY[q_plane, pl.ds(r0 - LO + 1, 8), :] = flux_y(q_plane, v_plane, r0)

    def combine(q_plane):
        for r0 in range(0, SPAN, 16):
            TEND[q_plane, pl.ds(r0, 16), :] = -(TEND[q_plane, pl.ds(r0, 16), :] + (
                FY[q_plane, pl.ds(r0 + 1, 16), :] - FY[q_plane, pl.ds(r0, 16), :]))

    def tracer_x(k, r0, n):
        q0, q1, gm2, gm1, g0, g1, g2 = x_parts(TS[k, pl.ds(PAD + r0, n), :])
        XU[k, pl.ds(r0, n), :] = q0 + correction(gm2, gm1, g0, g1)
        XD[k, pl.ds(r0, n), :] = q1 - correction(g2, g1, g0, gm1)

    def tracer_y(k, r0):
        q0, q1, gm2, gm1, g0, g1, g2 = y_parts(TS, k, PAD - 1 + r0, 8)
        YU[k, pl.ds(r0, 8), :] = q0 + correction(gm2, gm1, g0, g1)
        YD[k, pl.ds(r0, 8), :] = q1 - correction(g2, g1, g0, gm1)

    def local_part(k, carry):
        plane = lax.rem(k, LEVELS)
        for r0 in (16, 32):
            put_x(k, plane, r0, 16)
        for r0 in (23, 31):
            put_y(k, V_MAIN + plane, r0)
        for r0 in (0, 16):
            tracer_x(k, r0, 16)
        for r0 in (8, 16):
            tracer_y(k, r0)
        return carry

    lax.fori_loop(0, 8, local_part, 0)

    for d in (NORTH, SOUTH, EAST, NE, SE):
        send_to_later(d)

    @pl.when(far_b & later[NORTH])
    def _():
        to_hub.start()

    for d in (NORTH, SOUTH):
        wait_from(d)

    zero16 = jnp.zeros((16, COLS), F32)

    @pl.when(lat == 0)
    def _():
        for k in range(8):
            UV[k, under, :] = zero16
            TS[k, under, :] = zero16
        WE[0, under, :] = zero16
        WE[1, under, :] = zero16

    @pl.when(lat == n_lat - 1)
    def _():
        for k in range(8):
            UV[k, over, :] = zero16
            TS[k, over, :] = zero16
        WE[0, over, :] = zero16
        WE[1, over, :] = zero16

    def edge_part(k, carry):
        plane = lax.rem(k, LEVELS)
        for r0 in (8, 48):
            put_x(k, plane, r0, 8)
        for r0 in (7, 15, 39, 47):
            put_y(k, V_MAIN + plane, r0)
        combine(k)
        for r0 in (0, 24, 32):
            tracer_y(k, r0)
        return carry

    lax.fori_loop(0, 8, edge_part, 0)

    lane64 = lax.broadcasted_iota(jnp.int32, (EXT, COLS), 1)
    half = lax.rem(lane64, 32) < 16
    lane = lax.broadcasted_iota(jnp.int32, (SPAN, COLS), 1)
    level = (lane // 32).astype(F32)
    BAND = pl.ds(LO, SPAN)
    LOWER = pl.ds(LO - 1, SPAN)
    ALL = pl.ds(0, SPAN)
    scale = STEP / SUB
    own = slice(PAD - LO, PAD - LO + ROWS)

    def band(x):
        return x[LO:LO + SPAN]

    def joined(sw, main, se):
        return jnp.where(lane < 24, sw, jnp.where(lane < 64, lanes(main, 16), jnp.where(lane < 104, lanes(main, -16), se)))

    def faces(w):
        at = band(w)
        return jnp.minimum(at, lanes(at, -1)), jnp.minimum(at, band(rows(w, -1)))

    def main_sum(ref, first, where_rows, limit=None):
        total = None
        for k in range(LEVELS):
            term = ref[first + k, where_rows, :]
            if limit is not None:
                term = jnp.where(limit > k, term, 0.0)
            total = term if total is None else total + term
        return total

    def side_sum(ref, plane, where_rows, limit=None):
        term = ref[plane, where_rows, :]
        if limit is not None:
            term = jnp.where(limit > level, term, 0.0)
        return level_sum(term)

    def substeps(height, tx, ty, tym, fx, fy, cx, cy):
        for n in range(SUB):
            below = tym if n == 0 else rows(ty, 1)
            height = height - (tx - lanes(tx, 1) + ty - below)
            tx = tx - cx * (lanes(height, -1) - height) + fx
            ty = ty - cy * (rows(height, -1) - height) + fy
        return height, tx, ty

    wx_main, wy_main = faces(WE[0])
    push_x = main_sum(TEND, U_MAIN, ALL, wx_main)
    push_y = main_sum(TEND, V_MAIN, ALL, wy_main)
    tx0 = main_sum(UV, U_MAIN, BAND)
    ty0 = main_sum(UV, V_MAIN, BAND)
    tym_main = main_sum(UV, V_MAIN, LOWER)
    h_main, tx_main, ty_main = substeps(
        WE[1, BAND, :], tx0, ty0, tym_main, scale * push_x, scale * push_y, WAVE * wx_main, WAVE * wy_main)
    gain_x = (tx_main - (tx0 + STEP * push_x)) / jnp.maximum(wx_main, 1.0)
    gain_y = (ty_main - (ty0 + STEP * push_y)) / jnp.maximum(wy_main, 1.0)
    for k in range(LEVELS):
        NU[k] = jnp.where(wx_main > k, UV[U_MAIN + k, BAND, :] + STEP * TEND[U_MAIN + k, ALL, :] + gain_x, 0.0)[own]
        NV[k] = jnp.where(wy_main > k, UV[V_MAIN + k, BAND, :] + STEP * TEND[V_MAIN + k, ALL, :] + gain_y, 0.0)
    for slot, plane in enumerate((
            h_main, joined(tx0, tx0, tx0), joined(ty0, ty0, ty0), joined(tym_main, tym_main, tym_main),
            joined(push_x, push_x, push_x), joined(push_y, push_y, push_y),
            joined(wx_main, wx_main, wx_main), joined(wy_main, wy_main, wy_main))):
        KEPT[slot] = plane
    rings = [ring([UV[first + k] for k in range(LEVELS)]) for first in (U_MAIN, V_MAIN)]
    UV[U_SW] = rings[0]
    UV[V_SW] = rings[1]

    for d in (WEST, NW, SW):
        send_to_later(d)

    @pl.when(hub)
    def _():
        to_hub.wait_recv()
        hub_west.start()

    wait_from(EAST)

    @pl.when(hub)
    def _():
        hub_south.start()

    for d in (WEST, NE, SE, NW, SW):
        wait_from(d)

    @pl.when(lat == 0)
    def _():
        for i in range(2):
            RW[i, under, :] = zero16
            RE[i, under, :] = zero16

    @pl.when(lat == n_lat - 1)
    def _():
        for i in range(2):
            RW[i, over, :] = zero16
            RE[i, over, :] = zero16

    ring_u, ring_v = UV[U_SW], UV[V_SW]
    UV[U_SE] = jnp.where(half, ring_u, lanes(RE[0], 16))
    UV[V_SE] = jnp.where(half, ring_v, RE[0])
    UV[U_SW] = jnp.where(half, RW[0], ring_u)
    UV[V_SW] = jnp.where(half, lanes(RW[0], -16), ring_v)

    def strips(i, carry):
        for q_plane in (U_SW + i, V_SW + i):
            for r0 in (8, 24, 40):
                put_x(q_plane, U_SW + i, r0, 16)
            for r0 in (7, 15, 23, 31, 39, 47):
                put_y(q_plane, V_SW + i, r0)
            combine(q_plane)
        return carry

    lax.fori_loop(0, 2, strips, 0)

    def kept(slot, sw, se):
        return jnp.where(lane < 24, sw, jnp.where(lane >= 104, se, KEPT[slot]))

    wet_own = lanes(WE[0], 16)
    wx_sw, wy_sw = faces(spread(jnp.where(lane64 < 16, lanes(RW[1], -8), wet_own), 0))
    wx_se, wy_se = faces(spread(jnp.where(lane64 < 16, wet_own, lanes(RE[1], -8)), 0))
    eta_main = WE[1, BAND, :]
    eta_own = lanes(eta_main, 16)
    eta_side = joined(spread(jnp.where(lane < 16, lanes(RW[1, BAND, :], 8), eta_own), 0), eta_main,
                      spread(jnp.where(lane < 16, eta_own, lanes(RE[1, BAND, :], 8)), 0))

    push_x_sw = side_sum(TEND, U_SW, ALL, wx_sw)
    push_x_se = side_sum(TEND, U_SE, ALL, wx_se)
    push_y_sw = side_sum(TEND, V_SW, ALL, wy_sw)
    push_y_se = side_sum(TEND, V_SE, ALL, wy_se)
    tx0_sw, tx0_se = side_sum(UV, U_SW, BAND), side_sum(UV, U_SE, BAND)
    ty0_sw, ty0_se = side_sum(UV, V_SW, BAND), side_sum(UV, V_SE, BAND)

    h_side, tx_side, ty_side = substeps(
        eta_side, kept(1, tx0_sw, tx0_se), kept(2, ty0_sw, ty0_se),
        kept(3, side_sum(UV, V_SW, LOWER), side_sum(UV, V_SE, LOWER)),
        scale * kept(4, push_x_sw, push_x_se), scale * kept(5, push_y_sw, push_y_se),
        WAVE * kept(6, wx_sw, wx_se), WAVE * kept(7, wy_sw, wy_se))

    result[16] = jnp.where(lane < 16, lanes(h_side, -16), jnp.where(lane >= 112, lanes(h_side, 16), KEPT[0]))[own]

    def fresh_side(plane, trans0, push, depth, trans):
        step = UV[plane, BAND, :] + STEP * TEND[plane, ALL, :]
        return jnp.where(depth > level, step + (trans - (trans0 + STEP * push)) / jnp.maximum(depth, 1.0), 0.0)

    u_sw = fresh_side(U_SW, tx0_sw, push_x_sw, wx_sw, spread(tx_side, 0))[own]
    u_se = fresh_side(U_SE, tx0_se, push_x_se, wx_se, spread(tx_side, 96))[own]
    v_sw = fresh_side(V_SW, ty0_sw, push_y_sw, wy_sw, spread(ty_side, 0))
    v_se = fresh_side(V_SE, ty0_se, push_y_se, wy_se, spread(ty_side, 96))

    for k in range(LEVELS):
        fresh = jnp.where(lane32 < 12, lanes(u_sw, -(32 * k + 16)), jnp.where(lane32 >= 116, lanes(u_se, 112 - 32 * k), NU[k]))
        NU[k] = fresh
        result[k] = fresh
        fresh = jnp.where(lane < 12, lanes(v_sw, -(32 * k + 16)), jnp.where(lane >= 116, lanes(v_se, 112 - 32 * k), NV[k]))
        NV[k] = fresh
        result[4 + k] = fresh[own]

    ring_t = ring([TS[k, OWN, :] for k in range(LEVELS)])
    ring_s = ring([TS[4 + k, OWN, :] for k in range(LEVELS)])

    def side_flux(cells, flow):
        flux = flow * upwind_value(flow, *x_parts(cells))
        return flux - lanes(flux, 1)

    XS[0] = side_flux(jnp.where(half32, RW[1, OWN, :], ring_t), u_sw)
    XS[1] = side_flux(jnp.where(half32, ring_t, lanes(RE[1, OWN, :], 16)), u_se)
    XS[2] = side_flux(jnp.where(half32, lanes(RW[1, OWN, :], -16), ring_s), u_sw)
    XS[3] = side_flux(jnp.where(half32, ring_s, RE[1, OWN, :]), u_se)

    for field in range(2):
        for k in range(LEVELS):
            p = 4 * field + k
            flow = NU[k]
            flux = flow * jnp.where(flow >= 0.0, XU[p], XD[p])
            div_x = flux - lanes(flux, 1)
            div_x = jnp.where(lane32 < 8, lanes(XS[2 * field], -(32 * k + 16)),
                              jnp.where(lane32 >= 120, lanes(XS[2 * field + 1], 112 - 32 * k), div_x))
            up = NV[k, pl.ds(8, ROWS), :]
            down = NV[k, pl.ds(7, ROWS), :]
            flux_up = up * jnp.where(up >= 0.0, YU[p, pl.ds(1, ROWS), :], YD[p, pl.ds(1, ROWS), :])
            flux_down = down * jnp.where(down >= 0.0, YU[p, pl.ds(0, ROWS), :], YD[p, pl.ds(0, ROWS), :])
            cells = TS[p, OWN, :]
            fresh = cells - STEP * (div_x + (flux_up - flux_down))
            result[8 + p] = jnp.where(wet[0] > k, fresh, 0.0)

    for d in range(8):
        if d in (SE, NW):
            @pl.when(earlier[d] | later[d])
            def _():
                for copy in copies(d):
                    copy.wait_send()
        else:
            for copy in copies(d):
                copy.wait_send()

    @pl.when(hub)
    def _():
        hub_west.wait_send()
        hub_south.wait_send()

    @pl.when(far_b)
    def _():
        to_hub.wait_send()


def deal(result, u_out, v_out, t_out, s_out, e_out):
    for i, out in enumerate((u_out, v_out, t_out, s_out)):
        for k in range(LEVELS):
            out[k] = result[LEVELS * i + k]
    e_out[...] = result[16]


def solution(mesh):
    n_lat, n_lon = mesh.shape["lat"], mesh.shape["lon"]

    def step(u_vel, v_vel, temp, salt, eta, wet_levels):
        levels = jax.ShapeDtypeStruct((LEVELS, ROWS, COLS), F32)
        plane = jax.ShapeDtypeStruct((ROWS, COLS), F32)
        hbm = pl.BlockSpec(memory_space=pl.ANY)
        vmem = pl.BlockSpec(memory_space=pltpu.VMEM)

        def body(*refs):
            kernel(n_lat, n_lon, *refs)

        def buffer(*shape):
            return pltpu.VMEM(shape, F32)

        result = pl.pallas_call(
            body,
            out_shape=jax.ShapeDtypeStruct((17, ROWS, COLS), F32),
            in_specs=[hbm] * 6,
            out_specs=vmem,
            scratch_shapes=[
                buffer(16, ROWS, COLS),
                buffer(ROWS, COLS),
                pltpu.VMEM((3, ROWS, COLS), jnp.int32),
                buffer(12, EXT, COLS),
                buffer(8, EXT, COLS),
                buffer(2, EXT, COLS),
                buffer(2, EXT, COLS),
                buffer(2, EXT, COLS),
                buffer(2, EXT, COLS),
                buffer(2, EXT, COLS),
                buffer(2, PAD, COLS),
                buffer(8, SPAN, COLS),
                buffer(12, SPAN, COLS),
                buffer(12, SPAN + 8, COLS),
                buffer(8, ROWS, COLS),
                buffer(8, ROWS, COLS),
                buffer(8, 40, COLS),
                buffer(8, 40, COLS),
                buffer(4, SPAN, COLS),
                buffer(4, ROWS, COLS),
                buffer(4, ROWS, COLS),
                pltpu.SemaphoreType.DMA((6,)),
                pltpu.SemaphoreType.REGULAR((8,)),
                pltpu.SemaphoreType.DMA((15,)),
                pltpu.SemaphoreType.DMA((15,)),
            ],
            compiler_params=pltpu.CompilerParams(collective_id=0, has_side_effects=True),
        )(u_vel, v_vel, temp, salt, eta, wet_levels)
        return pl.pallas_call(
            deal,
            out_shape=(levels, levels, levels, levels, plane),
            in_specs=[vmem],
            out_specs=(vmem,) * 5,
        )(result)

    tile, flat = P(None, "lat", "lon"), P("lat", "lon")
    return jax.shard_map(
        step, mesh=mesh, in_specs=(tile, tile, tile, tile, flat, tile),
        out_specs=(tile, tile, tile, tile, flat), check_vma=False)
```

time: 44.1 us -> 44.8 us (1.016)
  the two profiles are of different devices: /device:TPU:998 before, /device:TPU:25 now
where the time goes in v3:
time: 44.8 us; the launch traced here: 44.6 us
  Pallas kernels  43.9 us (98%)
  between operations  0.64 us (1%)
    pallas_call x1, Pallas kernels, step(): pl.pallas_call(body, out_shape=jax.ShapeDtypeStruct((17, ROWS, COLS), F32...  42.3 us
    pallas_call x1, Pallas kernels, step(): pl.pallas_call(deal, out_shape=(levels, levels, levels, levels, plane), i...  1.66 us

profile of v3, /device:TPU:25, one launch (start us, length us, event | category | flops | bytes accessed | tf_op | source)
XLA Modules:
  0.0 44.6 jit_solution(13528970175920682674)
XLA Ops:
  0.6 42.3 %shard_map.101.result = f32[17,32,128]{2,1,0:T(8,128)} custom-call(f32[4,32,128]{2,1,0:T(8,128)} %refs_0_.1, f32[4,32,128]{2,1,0:T(8,128)} %refs_1_.1, f32[4,32,128]{2,1,0:T(8,128)} %refs_2_.1, f32[4,32,128]{2,1,0:T(8,128)} %refs_3_.1, f32[32,128]{1,0:T(8,128)} %refs_4_.1, s32[3,32,128]{2,1,0:T(8,128)} %refs_5_.1), custom_call_target="tpu_custom_call" | custom-call | tf_op jit(solution)/shard_map/pallas_call | solution.py:548
  42.9 1.7 %shard_map.102 = (f32[4,32,128]{2,1,0:T(8,128)}, f32[4,32,128]{2,1,0:T(8,128)}, f32[4,32,128]{2,1,0:T(8,128)}, f32[4,32,128]{2,1,0:T(8,128)}, f32[32,128]{1,0:T(8,128)}) custom-call(f32[17,32,128]{2,1,0:T(8,128)} %shard_map.101.result), custom_call_target="tpu_custom_call" | custom-call | tf_op jit(solution)/shard_map/pallas_call | solution.py:582

commit v4 on v3

--- a/solution.py
+++ b/solution.py
@@ -10,6 +10,7 @@
 LEVELS = 4
 SUB = 8
 BLOCK = 8
+RELAYED_FROM = 2
 STEP = 0.4
 WAVE = 0.45 / 4
 EPS = 1e-6 * 12.0 / 13.0
@@ -105,16 +106,18 @@
     def start_rank(i, j):
         group = j // BLOCK
         group = jnp.where(group == 2, 3, jnp.where(group == 3, 2, group))
-        return (group * BLOCK + lax.rem(i, BLOCK)) * (n_lat * n_lon) + i * n_lon + j
+        rank = (group * BLOCK + lax.rem(i, BLOCK)) * (n_lat * n_lon) + i * n_lon + j
+        return jnp.where((i == 0) & (j == 0), 2 * BLOCK * n_lat * n_lon - 1, rank)
 
     peers = [(lax.rem(lat + n_lat + di, n_lat), lax.rem(lon + n_lon + dj, n_lon)) for di, dj in DIRS]
     here = start_rank(lat, lon)
     earlier = [start_rank(*peer) < here for peer in peers]
     first_row, last_row = lax.rem(lat, BLOCK) == 0, lax.rem(lat, BLOCK) == BLOCK - 1
     first_column, last_column = lax.rem(lon, BLOCK) == 0, lax.rem(lon, BLOCK) == BLOCK - 1
-    far_a = first_row & last_column
-    far_b = last_row & first_column
-    hub = first_row & first_column
+    west_relayed = peers[WEST][1] // BLOCK >= RELAYED_FROM
+    far_a = first_row & last_column & (lon // BLOCK >= RELAYED_FROM)
+    far_b = last_row & first_column & west_relayed
+    hub = first_row & first_column & west_relayed
     later = [jnp.logical_not(flag) for flag in earlier]
     for d, far in ((SE, far_a), (NW, far_b)):
         earlier[d] = earlier[d] & jnp.logical_not(far)
@@ -200,8 +203,8 @@
             for copy in copies(d):
                 copy.start()
 
-    def send_to_later(d):
-        @pl.when(later[d])
+    def send_to_later(d, also=True):
+        @pl.when(later[d] & also)
         def _():
             pl.semaphore_wait(ready.at[d], 1)
             for copy in copies(d):
@@ -280,8 +283,13 @@
 
     lax.fori_loop(0, 8, local_part, 0)
 
-    for d in (NORTH, SOUTH, EAST, NE, SE):
+    send_to_later(NORTH)
+    for d in (EAST, NE):
+        send_to_later(d, jnp.logical_not(last_column))
+    for d in (SOUTH, SE):
         send_to_later(d)
+    for d in (EAST, NE):
+        send_to_later(d, last_column)
 
     @pl.when(far_b & later[NORTH])
     def _():
@@ -523,11 +531,14 @@
         to_hub.wait_send()
 
 
-def deal(result, u_out, v_out, t_out, s_out, e_out):
-    for i, out in enumerate((u_out, v_out, t_out, s_out)):
-        for k in range(LEVELS):
-            out[k] = result[LEVELS * i + k]
-    e_out[...] = result[16]
+def deal(result, u_out, v_out, t_out, s_out, e_out, sem):
+    copies = [pltpu.make_async_copy(result.at[pl.ds(LEVELS * i, LEVELS)], out, sem.at[i])
+              for i, out in enumerate((u_out, v_out, t_out, s_out))]
+    copies.append(pltpu.make_async_copy(result.at[16], e_out, sem.at[4]))
+    for copy in copies:
+        copy.start()
+    for copy in copies:
+        copy.wait()
 
 
 def solution(mesh):
@@ -547,7 +558,7 @@
 
         result = pl.pallas_call(
             body,
-            out_shape=jax.ShapeDtypeStruct((17, ROWS, COLS), F32),
+            out_shape=pltpu.VMEM((17, ROWS, COLS), F32),
             in_specs=[hbm] * 6,
             out_specs=vmem,
             scratch_shapes=[
@@ -583,7 +594,9 @@
             deal,
             out_shape=(levels, levels, levels, levels, plane),
             in_specs=[vmem],
-            out_specs=(vmem,) * 5,
+            out_specs=(hbm,) * 5,
+            scratch_shapes=[pltpu.SemaphoreType.DMA((5,))],
+            compiler_params=pltpu.CompilerParams(vmem_limit_bytes=1 << 20),
         )(result)
 
     tile, flat = P(None, "lat", "lon"), P("lat", "lon")

time: 44.8 us -> 37.7 us (0.84)
  the two profiles are of different devices: /device:TPU:25 before, /device:TPU:56 now
where the time goes in v4:
time: 37.7 us; the launch traced here: 37.5 us
  Pallas kernels  36.8 us (98%)
  between operations  0.64 us (2%)
    pallas_call x1, Pallas kernels, step(): pl.pallas_call(body, out_shape=pltpu.VMEM((17, ROWS, COLS), F32), in_spec...  36.1 us

profile of v4, /device:TPU:56, one launch (start us, length us, event | category | flops | bytes accessed | tf_op | source)
XLA Modules:
  0.0 37.5 jit_solution(13442065830086488567)
XLA Ops:
  0.6 36.1 %shard_map.101.result = f32[17,32,128]{2,1,0:T(8,128)S(1)} custom-call(f32[4,32,128]{2,1,0:T(8,128)} %refs_0_.1, f32[4,32,128]{2,1,0:T(8,128)} %refs_1_.1, f32[4,32,128]{2,1,0:T(8,128)} %refs_2_.1, f32[4,32,128]{2,1,0:T(8,128)} %refs_3_.1, f32[32,128]{1,0:T(8,128)} %refs_4_.1, s32[3,32,128]{2,1,0:T(8,128)} %refs_5_.1), custom_call_target="tpu_custom_call" | custom-call | tf_op jit(solution)/shard_map/pallas_call | solution.py:559
  36.7 0.7 %shard_map.102 = (f32[4,32,128]{2,1,0:T(8,128)}, f32[4,32,128]{2,1,0:T(8,128)}, f32[4,32,128]{2,1,0:T(8,128)}, f32[4,32,128]{2,1,0:T(8,128)}, f32[32,128]{1,0:T(8,128)}) custom-call(f32[17,32,128]{2,1,0:T(8,128)S(1)} %shard_map.101.result), custom_call_target="tpu_custom_call" | custom-call | tf_op jit(solution)/shard_map/pallas_call | solution.py:593

commit v5 on v4

--- a/solution.py
+++ b/solution.py
@@ -114,14 +114,15 @@
     earlier = [start_rank(*peer) < here for peer in peers]
     first_row, last_row = lax.rem(lat, BLOCK) == 0, lax.rem(lat, BLOCK) == BLOCK - 1
     first_column, last_column = lax.rem(lon, BLOCK) == 0, lax.rem(lon, BLOCK) == BLOCK - 1
+    inner_west, inner_east = jnp.logical_not(first_column), jnp.logical_not(last_column)
+    relayed = lon // BLOCK >= RELAYED_FROM
     west_relayed = peers[WEST][1] // BLOCK >= RELAYED_FROM
-    far_a = first_row & last_column & (lon // BLOCK >= RELAYED_FROM)
-    far_b = last_row & first_column & west_relayed
-    hub = first_row & first_column & west_relayed
+    corner_a, corner_b, corner_hub = first_row & last_column, last_row & first_column, first_row & first_column
     later = [jnp.logical_not(flag) for flag in earlier]
-    for d, far in ((SE, far_a), (NW, far_b)):
-        earlier[d] = earlier[d] & jnp.logical_not(far)
-        later[d] = later[d] & jnp.logical_not(far)
+    earlier[SE] = earlier[SE] & jnp.logical_not(corner_a)
+    later[SE] = later[SE] & jnp.logical_not(corner_a)
+    earlier[NW] = (earlier[NW] & jnp.logical_not(corner_b)) | (corner_b & jnp.logical_not(west_relayed))
+    later[NW] = later[NW] & jnp.logical_not(corner_b)
 
     barrier = pltpu.get_barrier_semaphore()
     expected = 0
@@ -131,6 +132,10 @@
         @pl.when(later[d])
         def _():
             pl.semaphore_signal(barrier, inc=1, device_id=peers[d], device_id_type=MESH)
+
+    @pl.when(corner_a & jnp.logical_not(relayed))
+    def _():
+        pl.semaphore_signal(barrier, inc=1, device_id=peers[SE], device_id_type=MESH)
 
     loads = [
         pltpu.make_async_copy(w_hbm, wet, in_sem.at[0]),
@@ -197,8 +202,8 @@
                 device_id=peers[d], device_id_type=MESH)
             for i, (src, dst) in enumerate(parcels[d])]
 
-    def send_to_earlier(d):
-        @pl.when(earlier[d])
+    def send_to_earlier(d, also=True):
+        @pl.when(earlier[d] & also)
         def _():
             for copy in copies(d):
                 copy.start()
@@ -228,14 +233,18 @@
         pl.semaphore_wait(barrier, expected)
 
     for d in range(8):
-        @pl.when(earlier[d])
+        @pl.when(earlier[d] & jnp.logical_not(corner_b) if d == NW else earlier[d])
         def _():
             pl.semaphore_signal(ready.at[DIRS.index((-DIRS[d][0], -DIRS[d][1]))], inc=1, device_id=peers[d], device_id_type=MESH)
 
-    for d in (EAST, NE, SE, WEST, NW, SW, NORTH, SOUTH):
+    send_to_earlier(NW, corner_b)
+    for d in (EAST, NE, SE, WEST, SW):
         send_to_earlier(d)
-
-    @pl.when(far_b & earlier[NORTH])
+    send_to_earlier(NW, jnp.logical_not(corner_b))
+    for d in (NORTH, SOUTH):
+        send_to_earlier(d)
+
+    @pl.when(corner_b & west_relayed & earlier[NORTH])
     def _():
         to_hub.start()
 
@@ -284,16 +293,20 @@
     lax.fori_loop(0, 8, local_part, 0)
 
     send_to_later(NORTH)
-    for d in (EAST, NE):
-        send_to_later(d, jnp.logical_not(last_column))
-    for d in (SOUTH, SE):
-        send_to_later(d)
-    for d in (EAST, NE):
+
+    @pl.when(corner_b & west_relayed & later[NORTH])
+    def _():
+        to_hub.start()
+
+    send_to_later(EAST, inner_east)
+    send_to_later(NE, inner_east)
+    send_to_later(WEST, inner_west)
+    send_to_later(NW, inner_west)
+    send_to_later(SOUTH)
+    send_to_later(SE, inner_east)
+    send_to_later(SW, inner_west)
+    for d in (EAST, NE, SE):
         send_to_later(d, last_column)
-
-    @pl.when(far_b & later[NORTH])
-    def _():
-        to_hub.start()
 
     for d in (NORTH, SOUTH):
         wait_from(d)
@@ -395,16 +408,16 @@
     UV[V_SW] = rings[1]
 
     for d in (WEST, NW, SW):
-        send_to_later(d)
-
-    @pl.when(hub)
+        send_to_later(d, first_column)
+
+    @pl.when(corner_hub & west_relayed)
     def _():
         to_hub.wait_recv()
         hub_west.start()
 
     wait_from(EAST)
 
-    @pl.when(hub)
+    @pl.when(corner_hub)
     def _():
         hub_south.start()
 
@@ -521,12 +534,15 @@
             for copy in copies(d):
                 copy.wait_send()
 
-    @pl.when(hub)
+    @pl.when(corner_hub)
+    def _():
+        hub_south.wait_send()
+
+    @pl.when(corner_hub & west_relayed)
     def _():
         hub_west.wait_send()
-        hub_south.wait_send()
-
-    @pl.when(far_b)
+
+    @pl.when(corner_b & west_relayed)
     def _():
         to_hub.wait_send()
 

time: 37.7 us -> 35.3 us (0.936)
  the two profiles are of different devices: /device:TPU:56 before, /device:TPU:230 now
where the time goes in v5:
time: 35.3 us; the launch traced here: 35 us
  Pallas kernels  34.4 us (97%)
  between operations  0.64 us (2%)
    pallas_call x1, Pallas kernels, step(): pl.pallas_call(body, out_shape=pltpu.VMEM((17, ROWS, COLS), F32), in_spec...  33.7 us
    pallas_call x1, Pallas kernels, step(): pl.pallas_call(deal, out_shape=(levels, levels, levels, levels, plane), i...  0.74 us

profile of v5, /device:TPU:230, one launch (start us, length us, event | category | flops | bytes accessed | tf_op | source)
XLA Modules:
  0.0 35.0 jit_solution(6730104246701231451)
XLA Ops:
  0.6 33.7 %shard_map.101.result = f32[17,32,128]{2,1,0:T(8,128)S(1)} custom-call(f32[4,32,128]{2,1,0:T(8,128)} %refs_0_.1, f32[4,32,128]{2,1,0:T(8,128)} %refs_1_.1, f32[4,32,128]{2,1,0:T(8,128)} %refs_2_.1, f32[4,32,128]{2,1,0:T(8,128)} %refs_3_.1, f32[32,128]{1,0:T(8,128)} %refs_4_.1, s32[3,32,128]{2,1,0:T(8,128)} %refs_5_.1), custom_call_target="tpu_custom_call" | custom-call | tf_op jit(solution)/shard_map/pallas_call | solution.py:575
  34.3 0.7 %shard_map.102 = (f32[4,32,128]{2,1,0:T(8,128)}, f32[4,32,128]{2,1,0:T(8,128)}, f32[4,32,128]{2,1,0:T(8,128)}, f32[4,32,128]{2,1,0:T(8,128)}, f32[32,128]{1,0:T(8,128)}) custom-call(f32[17,32,128]{2,1,0:T(8,128)S(1)} %shard_map.101.result), custom_call_target="tpu_custom_call" | custom-call | tf_op jit(solution)/shard_map/pallas_call | solution.py:609

commit v6 on v5

--- a/solution.py
+++ b/solution.py
@@ -97,7 +97,7 @@
 
 def kernel(n_lat, n_lon, u_hbm, v_hbm, t_hbm, s_hbm, e_hbm, w_hbm,
            result,
-           raw, raw2, wet, UV, TS, WE, PE, PW, RW, RE, HUB, KEPT,
+           raw, raw2, wet, UV, TS, WE, PE, PW, RW, RE, HUB, KEPT, RINGS,
            TEND, FY, XU, XD, YU, YD, NV, NU, XS,
            in_sem, ready, send_sem, recv_sem):
     lat = lax.axis_index("lat")
@@ -165,14 +165,18 @@
     ring_v = ring([UV[V_MAIN + k, OWN, :] for k in range(LEVELS)])
     ring_t = ring([TS[k, OWN, :] for k in range(LEVELS)])
     ring_s = ring([TS[4 + k, OWN, :] for k in range(LEVELS)])
-    eta8, wet24 = lanes(raw2[...], 8), lanes(wet[0].astype(F32), 24)
+    eta8 = lanes(raw2[...], 8)
+    wet8 = lanes(ring([wet[0].astype(F32)] * LEVELS), 8)
+    spot = lax.rem(lane32, 32)
     PE[0, OWN, :] = jnp.where(half32, ring_u, lanes(ring_v, 16))
     PW[0, OWN, :] = jnp.where(half32, lanes(ring_u, -16), ring_v)
     PE[1, OWN, :] = jnp.where(lane32 < 8, eta8, jnp.where(
-        (lane32 >= 16) & (lane32 < 24), wet24, jnp.where(half32, ring_t, lanes(ring_s, 16))))
+        (spot >= 16) & (spot < 24), wet8, jnp.where(half32, ring_t, lanes(ring_s, 16))))
     PW[1, OWN, :] = jnp.where((lane32 >= 8) & (lane32 < 16), eta8, jnp.where(
-        (lane32 >= 24) & (lane32 < 32), wet24, jnp.where(half32, lanes(ring_t, -16), ring_s)))
-
+        spot >= 24, wet8, jnp.where(half32, lanes(ring_t, -16), ring_s)))
+
+    RINGS[0, pl.ds(0, ROWS), :] = ring_t
+    RINGS[1, pl.ds(0, ROWS), :] = ring_s
     top, bottom = pl.ds(32, 16), pl.ds(16, 16)
     under, over = pl.ds(0, 16), pl.ds(48, 16)
     every = pl.ds(0, 8)
@@ -355,8 +359,8 @@
     def band(x):
         return x[LO:LO + SPAN]
 
-    def joined(sw, main, se):
-        return jnp.where(lane < 24, sw, jnp.where(lane < 64, lanes(main, 16), jnp.where(lane < 104, lanes(main, -16), se)))
+    def laid(main):
+        return jnp.where(lane < 48, lanes(main, 16), lanes(main, -48))
 
     def faces(w):
         at = band(w)
@@ -371,11 +375,10 @@
             total = term if total is None else total + term
         return total
 
-    def side_sum(ref, plane, where_rows, limit=None):
-        term = ref[plane, where_rows, :]
-        if limit is not None:
-            term = jnp.where(limit > level, term, 0.0)
-        return level_sum(term)
+    def pair_sum(sw, se):
+        low = lane < 64
+        folded = jnp.where(low, sw, se) + lanes(jnp.where(low, se, sw), 64)
+        return folded + lanes(folded, -32)
 
     def substeps(height, tx, ty, tym, fx, fy, cx, cy):
         for n in range(SUB):
@@ -398,14 +401,55 @@
     for k in range(LEVELS):
         NU[k] = jnp.where(wx_main > k, UV[U_MAIN + k, BAND, :] + STEP * TEND[U_MAIN + k, ALL, :] + gain_x, 0.0)[own]
         NV[k] = jnp.where(wy_main > k, UV[V_MAIN + k, BAND, :] + STEP * TEND[V_MAIN + k, ALL, :] + gain_y, 0.0)
-    for slot, plane in enumerate((
-            h_main, joined(tx0, tx0, tx0), joined(ty0, ty0, ty0), joined(tym_main, tym_main, tym_main),
-            joined(push_x, push_x, push_x), joined(push_y, push_y, push_y),
-            joined(wx_main, wx_main, wx_main), joined(wy_main, wy_main, wy_main))):
-        KEPT[slot] = plane
-    rings = [ring([UV[first + k] for k in range(LEVELS)]) for first in (U_MAIN, V_MAIN)]
-    UV[U_SW] = rings[0]
-    UV[V_SW] = rings[1]
+    KEPT[0] = h_main
+    for slot, plane in enumerate((tx0, ty0, tym_main, push_x, push_y, wx_main, wy_main, WE[1, BAND, :])):
+        KEPT[slot + 1] = laid(plane)
+    RINGS[2] = ring([UV[U_MAIN + k] for k in range(LEVELS)])
+    RINGS[3] = ring([UV[V_MAIN + k] for k in range(LEVELS)])
+    RINGS[4] = ring([WE[0]] * LEVELS)
+
+    def clear_poles(ref):
+        @pl.when(lat == 0)
+        def _():
+            for i in range(2):
+                ref[i, under, :] = zero16
+
+        @pl.when(lat == n_lat - 1)
+        def _():
+            for i in range(2):
+                ref[i, over, :] = zero16
+
+    def strip(u_plane, v_plane):
+        def one(i, carry):
+            q_plane = u_plane + i * (v_plane - u_plane)
+            for r0 in (8, 24, 40):
+                put_x(q_plane, u_plane, r0, 16)
+            for r0 in (7, 15, 23, 31, 39, 47):
+                put_y(q_plane, v_plane, r0)
+            combine(q_plane)
+            return carry
+
+        lax.fori_loop(0, 2, one, 0)
+
+    def western_strip():
+        for d in (NE, SE):
+            wait_from(d)
+        clear_poles(RW)
+        UV[U_SW] = jnp.where(half, RW[0], RINGS[2])
+        UV[V_SW] = jnp.where(half, lanes(RW[0], -16), RINGS[3])
+        strip(U_SW, V_SW)
+
+    def eastern_strip():
+        for d in (WEST, NW, SW):
+            wait_from(d)
+        clear_poles(RE)
+        UV[U_SE] = jnp.where(half, RINGS[2], lanes(RE[0], 16))
+        UV[V_SE] = jnp.where(half, RINGS[3], RE[0])
+        strip(U_SE, V_SE)
+
+    @pl.when(first_column)
+    def _():
+        eastern_strip()
 
     for d in (WEST, NW, SW):
         send_to_later(d, first_column)
@@ -421,72 +465,48 @@
     def _():
         hub_south.start()
 
-    for d in (WEST, NE, SE, NW, SW):
-        wait_from(d)
-
-    @pl.when(lat == 0)
-    def _():
-        for i in range(2):
-            RW[i, under, :] = zero16
-            RE[i, under, :] = zero16
-
-    @pl.when(lat == n_lat - 1)
-    def _():
-        for i in range(2):
-            RW[i, over, :] = zero16
-            RE[i, over, :] = zero16
-
-    ring_u, ring_v = UV[U_SW], UV[V_SW]
-    UV[U_SE] = jnp.where(half, ring_u, lanes(RE[0], 16))
-    UV[V_SE] = jnp.where(half, ring_v, RE[0])
-    UV[U_SW] = jnp.where(half, RW[0], ring_u)
-    UV[V_SW] = jnp.where(half, lanes(RW[0], -16), ring_v)
-
-    def strips(i, carry):
-        for q_plane in (U_SW + i, V_SW + i):
-            for r0 in (8, 24, 40):
-                put_x(q_plane, U_SW + i, r0, 16)
-            for r0 in (7, 15, 23, 31, 39, 47):
-                put_y(q_plane, V_SW + i, r0)
-            combine(q_plane)
-        return carry
-
-    lax.fori_loop(0, 2, strips, 0)
-
-    def kept(slot, sw, se):
-        return jnp.where(lane < 24, sw, jnp.where(lane >= 104, se, KEPT[slot]))
-
-    wet_own = lanes(WE[0], 16)
-    wx_sw, wy_sw = faces(spread(jnp.where(lane64 < 16, lanes(RW[1], -8), wet_own), 0))
-    wx_se, wy_se = faces(spread(jnp.where(lane64 < 16, wet_own, lanes(RE[1], -8)), 0))
-    eta_main = WE[1, BAND, :]
-    eta_own = lanes(eta_main, 16)
-    eta_side = joined(spread(jnp.where(lane < 16, lanes(RW[1, BAND, :], 8), eta_own), 0), eta_main,
-                      spread(jnp.where(lane < 16, eta_own, lanes(RE[1, BAND, :], 8)), 0))
-
-    push_x_sw = side_sum(TEND, U_SW, ALL, wx_sw)
-    push_x_se = side_sum(TEND, U_SE, ALL, wx_se)
-    push_y_sw = side_sum(TEND, V_SW, ALL, wy_sw)
-    push_y_se = side_sum(TEND, V_SE, ALL, wy_se)
-    tx0_sw, tx0_se = side_sum(UV, U_SW, BAND), side_sum(UV, U_SE, BAND)
-    ty0_sw, ty0_se = side_sum(UV, V_SW, BAND), side_sum(UV, V_SE, BAND)
+    western_strip()
+
+    @pl.when(inner_west)
+    def _():
+        eastern_strip()
+
+    in_sw, in_se = lane < 24, (lane >= 72) & (lane < 96)
+
+    def kept(slot, sides):
+        return jnp.where(in_sw | in_se, sides, KEPT[slot])
+
+    wx_sw, wy_sw = faces(jnp.where(half, lanes(RW[1], -8), RINGS[4]))
+    wx_se, wy_se = faces(jnp.where(half, RINGS[4], lanes(RE[1], -8)))
+    wx_side = kept(6, jnp.where(lane < 64, wx_sw, wx_se))
+    wy_side = kept(7, jnp.where(lane < 64, wy_sw, wy_se))
+    eta_side = jnp.where(lane < 16, lanes(RW[1, BAND, :], 8), jnp.where(
+        (lane >= 80) & (lane < 88), lanes(RE[1, BAND, :], 72), KEPT[8]))
+
+    def masked(plane, limit):
+        return jnp.where(limit > level, TEND[plane, ALL, :], 0.0)
+
+    push_x_side = kept(4, pair_sum(masked(U_SW, wx_sw), masked(U_SE, wx_se)))
+    push_y_side = kept(5, pair_sum(masked(V_SW, wy_sw), masked(V_SE, wy_se)))
+    tx0_side = kept(1, pair_sum(UV[U_SW, BAND, :], UV[U_SE, BAND, :]))
+    ty0_side = kept(2, pair_sum(UV[V_SW, BAND, :], UV[V_SE, BAND, :]))
+    tym_side = kept(3, pair_sum(UV[V_SW, LOWER, :], UV[V_SE, LOWER, :]))
 
     h_side, tx_side, ty_side = substeps(
-        eta_side, kept(1, tx0_sw, tx0_se), kept(2, ty0_sw, ty0_se),
-        kept(3, side_sum(UV, V_SW, LOWER), side_sum(UV, V_SE, LOWER)),
-        scale * kept(4, push_x_sw, push_x_se), scale * kept(5, push_y_sw, push_y_se),
-        WAVE * kept(6, wx_sw, wx_se), WAVE * kept(7, wy_sw, wy_se))
-
-    result[16] = jnp.where(lane < 16, lanes(h_side, -16), jnp.where(lane >= 112, lanes(h_side, 16), KEPT[0]))[own]
-
-    def fresh_side(plane, trans0, push, depth, trans):
-        step = UV[plane, BAND, :] + STEP * TEND[plane, ALL, :]
-        return jnp.where(depth > level, step + (trans - (trans0 + STEP * push)) / jnp.maximum(depth, 1.0), 0.0)
-
-    u_sw = fresh_side(U_SW, tx0_sw, push_x_sw, wx_sw, spread(tx_side, 0))[own]
-    u_se = fresh_side(U_SE, tx0_se, push_x_se, wx_se, spread(tx_side, 96))[own]
-    v_sw = fresh_side(V_SW, ty0_sw, push_y_sw, wy_sw, spread(ty_side, 0))
-    v_se = fresh_side(V_SE, ty0_se, push_y_se, wy_se, spread(ty_side, 96))
+        eta_side, tx0_side, ty0_side, tym_side, scale * push_x_side, scale * push_y_side, WAVE * wx_side, WAVE * wy_side)
+
+    result[16] = jnp.where(lane < 16, lanes(h_side, -16), jnp.where(lane >= 112, lanes(h_side, 48), KEPT[0]))[own]
+
+    gain_x = (tx_side - (tx0_side + STEP * push_x_side)) / jnp.maximum(wx_side, 1.0)
+    gain_y = (ty_side - (ty0_side + STEP * push_y_side)) / jnp.maximum(wy_side, 1.0)
+
+    def fresh_side(plane, depth, gain):
+        return jnp.where(depth > level, UV[plane, BAND, :] + STEP * TEND[plane, ALL, :] + gain, 0.0)
+
+    u_sw = fresh_side(U_SW, wx_sw, spread(gain_x, 0))[own]
+    u_se = fresh_side(U_SE, wx_se, spread(gain_x, 64))[own]
+    v_sw = fresh_side(V_SW, wy_sw, spread(gain_y, 0))
+    v_se = fresh_side(V_SE, wy_se, spread(gain_y, 64))
 
     for k in range(LEVELS):
         fresh = jnp.where(lane32 < 12, lanes(u_sw, -(32 * k + 16)), jnp.where(lane32 >= 116, lanes(u_se, 112 - 32 * k), NU[k]))
@@ -496,8 +516,7 @@
         NV[k] = fresh
         result[4 + k] = fresh[own]
 
-    ring_t = ring([TS[k, OWN, :] for k in range(LEVELS)])
-    ring_s = ring([TS[4 + k, OWN, :] for k in range(LEVELS)])
+    ring_t, ring_s = RINGS[0, pl.ds(0, ROWS), :], RINGS[1, pl.ds(0, ROWS), :]
 
     def side_flux(cells, flow):
         flux = flow * upwind_value(flow, *x_parts(cells))
@@ -589,7 +608,8 @@
                 buffer(2, EXT, COLS),
                 buffer(2, EXT, COLS),
                 buffer(2, PAD, COLS),
-                buffer(8, SPAN, COLS),
+                buffer(9, SPAN, COLS),
+                buffer(5, EXT, COLS),
                 buffer(12, SPAN, COLS),
                 buffer(12, SPAN + 8, COLS),
                 buffer(8, ROWS, COLS),

time: 35.3 us -> 35.4 us (level)
  no operation moved by 1% of the time
where the time goes in v6:
time: 35.4 us; the launch traced here: 35.2 us
  Pallas kernels  34.6 us (98%)
  between operations  0.64 us (2%)
    pallas_call x1, Pallas kernels, step(): pl.pallas_call(body, out_shape=pltpu.VMEM((17, ROWS, COLS), F32), in_spec...  33.8 us
    pallas_call x1, Pallas kernels, step(): pl.pallas_call(deal, out_shape=(levels, levels, levels, levels, plane), i...  0.74 us

profile of v6, /device:TPU:230, one launch (start us, length us, event | category | flops | bytes accessed | tf_op | source)
XLA Modules:
  0.0 35.2 jit_solution(3375033125669384822)
XLA Ops:
  0.6 33.8 %shard_map.101.result = f32[17,32,128]{2,1,0:T(8,128)S(1)} custom-call(f32[4,32,128]{2,1,0:T(8,128)} %refs_0_.1, f32[4,32,128]{2,1,0:T(8,128)} %refs_1_.1, f32[4,32,128]{2,1,0:T(8,128)} %refs_2_.1, f32[4,32,128]{2,1,0:T(8,128)} %refs_3_.1, f32[32,128]{1,0:T(8,128)} %refs_4_.1, s32[3,32,128]{2,1,0:T(8,128)} %refs_5_.1), custom_call_target="tpu_custom_call" | custom-call | tf_op jit(solution)/shard_map/pallas_call | solution.py:594
  34.5 0.7 %shard_map.102 = (f32[4,32,128]{2,1,0:T(8,128)}, f32[4,32,128]{2,1,0:T(8,128)}, f32[4,32,128]{2,1,0:T(8,128)}, f32[4,32,128]{2,1,0:T(8,128)}, f32[32,128]{1,0:T(8,128)}) custom-call(f32[17,32,128]{2,1,0:T(8,128)S(1)} %shard_map.101.result), custom_call_target="tpu_custom_call" | custom-call | tf_op jit(solution)/shard_map/pallas_call | solution.py:629

commit v7 on v6

--- a/solution.py
+++ b/solution.py
@@ -100,6 +100,17 @@
            raw, raw2, wet, UV, TS, WE, PE, PW, RW, RE, HUB, KEPT, RINGS,
            TEND, FY, XU, XD, YU, YD, NV, NU, XS,
            in_sem, ready, send_sem, recv_sem):
+    loads = [
+        pltpu.make_async_copy(w_hbm, wet, in_sem.at[0]),
+        pltpu.make_async_copy(u_hbm, raw.at[pl.ds(0, 4)], in_sem.at[1]),
+        pltpu.make_async_copy(v_hbm, raw.at[pl.ds(4, 4)], in_sem.at[2]),
+        pltpu.make_async_copy(t_hbm, raw.at[pl.ds(8, 4)], in_sem.at[3]),
+        pltpu.make_async_copy(s_hbm, raw.at[pl.ds(12, 4)], in_sem.at[4]),
+        pltpu.make_async_copy(e_hbm, raw2, in_sem.at[5]),
+    ]
+    for load in loads:
+        load.start()
+
     lat = lax.axis_index("lat")
     lon = lax.axis_index("lon")
 
@@ -137,34 +148,17 @@
     def _():
         pl.semaphore_signal(barrier, inc=1, device_id=peers[SE], device_id_type=MESH)
 
-    loads = [
-        pltpu.make_async_copy(w_hbm, wet, in_sem.at[0]),
-        pltpu.make_async_copy(u_hbm, raw.at[pl.ds(0, 4)], in_sem.at[1]),
-        pltpu.make_async_copy(v_hbm, raw.at[pl.ds(4, 4)], in_sem.at[2]),
-        pltpu.make_async_copy(t_hbm, raw.at[pl.ds(8, 4)], in_sem.at[3]),
-        pltpu.make_async_copy(s_hbm, raw.at[pl.ds(12, 4)], in_sem.at[4]),
-        pltpu.make_async_copy(e_hbm, raw2, in_sem.at[5]),
-    ]
-    for load in loads:
-        load.start()
     for load in loads:
         load.wait()
 
     OWN = pl.ds(PAD, ROWS)
-    for k in range(LEVELS):
-        UV[U_MAIN + k, OWN, :] = jnp.where(wet[1] > k, raw[k], 0.0)
-        UV[V_MAIN + k, OWN, :] = jnp.where(wet[2] > k, raw[4 + k], 0.0)
-        TS[k, OWN, :] = jnp.where(wet[0] > k, raw[8 + k], 0.0)
-        TS[4 + k, OWN, :] = jnp.where(wet[0] > k, raw[12 + k], 0.0)
-    WE[0, OWN, :] = wet[0].astype(F32)
-    WE[1, OWN, :] = raw2[...]
+
+    def wetted(first, face):
+        return [jnp.where(wet[face] > k, raw[first + k], 0.0) for k in range(LEVELS)]
 
     lane32 = lax.broadcasted_iota(jnp.int32, (ROWS, COLS), 1)
     half32 = lax.rem(lane32, 32) < 16
-    ring_u = ring([UV[U_MAIN + k, OWN, :] for k in range(LEVELS)])
-    ring_v = ring([UV[V_MAIN + k, OWN, :] for k in range(LEVELS)])
-    ring_t = ring([TS[k, OWN, :] for k in range(LEVELS)])
-    ring_s = ring([TS[4 + k, OWN, :] for k in range(LEVELS)])
+    ring_u, ring_v, ring_t, ring_s = ring(wetted(0, 1)), ring(wetted(4, 2)), ring(wetted(8, 0)), ring(wetted(12, 0))
     eta8 = lanes(raw2[...], 8)
     wet8 = lanes(ring([wet[0].astype(F32)] * LEVELS), 8)
     spot = lax.rem(lane32, 32)
@@ -245,6 +239,13 @@
     for d in (EAST, NE, SE, WEST, SW):
         send_to_earlier(d)
     send_to_earlier(NW, jnp.logical_not(corner_b))
+
+    for first, face, planes in ((0, 1, UV), (4, 2, UV), (8, 0, TS), (12, 0, TS)):
+        for k, plane in enumerate(wetted(first, face)):
+            planes[first % 8 + k, OWN, :] = plane
+    WE[0, OWN, :] = wet[0].astype(F32)
+    WE[1, OWN, :] = raw2[...]
+
     for d in (NORTH, SOUTH):
         send_to_earlier(d)
 

time: 35.4 us -> 35.4 us (level)
  no operation moved by 1% of the time
where the time goes in v7:
time: 35.4 us; the launch traced here: 35.2 us
  Pallas kernels  34.6 us (98%)
  between operations  0.64 us (2%)
    pallas_call x1, Pallas kernels, step(): pl.pallas_call(body, out_shape=pltpu.VMEM((17, ROWS, COLS), F32), in_spec...  33.8 us
    pallas_call x1, Pallas kernels, step(): pl.pallas_call(deal, out_shape=(levels, levels, levels, levels, plane), i...  0.74 us

profile of v7, /device:TPU:230, one launch (start us, length us, event | category | flops | bytes accessed | tf_op | source)
XLA Modules:
  0.0 35.2 jit_solution(2207909225646393712)
XLA Ops:
  0.6 33.8 %shard_map.101.result = f32[17,32,128]{2,1,0:T(8,128)S(1)} custom-call(f32[4,32,128]{2,1,0:T(8,128)} %refs_0_.1, f32[4,32,128]{2,1,0:T(8,128)} %refs_1_.1, f32[4,32,128]{2,1,0:T(8,128)} %refs_2_.1, f32[4,32,128]{2,1,0:T(8,128)} %refs_3_.1, f32[32,128]{1,0:T(8,128)} %refs_4_.1, s32[3,32,128]{2,1,0:T(8,128)} %refs_5_.1), custom_call_target="tpu_custom_call" | custom-call | tf_op jit(solution)/shard_map/pallas_call | solution.py:595
  34.5 0.7 %shard_map.102 = (f32[4,32,128]{2,1,0:T(8,128)}, f32[4,32,128]{2,1,0:T(8,128)}, f32[4,32,128]{2,1,0:T(8,128)}, f32[4,32,128]{2,1,0:T(8,128)}, f32[32,128]{1,0:T(8,128)}) custom-call(f32[17,32,128]{2,1,0:T(8,128)S(1)} %shard_map.101.result), custom_call_target="tpu_custom_call" | custom-call | tf_op jit(solution)/shard_map/pallas_call | solution.py:630

commit v8 on v7

--- a/solution.py
+++ b/solution.py
@@ -384,9 +384,9 @@
     def substeps(height, tx, ty, tym, fx, fy, cx, cy):
         for n in range(SUB):
             below = tym if n == 0 else rows(ty, 1)
-            height = height - (tx - lanes(tx, 1) + ty - below)
-            tx = tx - cx * (lanes(height, -1) - height) + fx
-            ty = ty - cy * (rows(height, -1) - height) + fy
+            height = height - (tx - lanes(tx, 1) + (ty - below))
+            tx = (tx + fx) - cx * (lanes(height, -1) - height)
+            ty = (ty + fy) - cy * (rows(height, -1) - height)
         return height, tx, ty
 
     wx_main, wy_main = faces(WE[0])

time: 35.4 us -> 35.4 us (level)
  no operation moved by 1% of the time
where the time goes in v8:
time: 35.4 us; the launch traced here: 35.2 us
  Pallas kernels  34.6 us (98%)
  between operations  0.64 us (2%)
    pallas_call x1, Pallas kernels, step(): pl.pallas_call(body, out_shape=pltpu.VMEM((17, ROWS, COLS), F32), in_spec...  33.8 us
    pallas_call x1, Pallas kernels, step(): pl.pallas_call(deal, out_shape=(levels, levels, levels, levels, plane), i...  0.74 us

profile of v8, /device:TPU:230, one launch (start us, length us, event | category | flops | bytes accessed | tf_op | source)
XLA Modules:
  0.0 35.2 jit_solution(826499050891197962)
XLA Ops:
  0.6 33.8 %shard_map.101.result = f32[17,32,128]{2,1,0:T(8,128)S(1)} custom-call(f32[4,32,128]{2,1,0:T(8,128)} %refs_0_.1, f32[4,32,128]{2,1,0:T(8,128)} %refs_1_.1, f32[4,32,128]{2,1,0:T(8,128)} %refs_2_.1, f32[4,32,128]{2,1,0:T(8,128)} %refs_3_.1, f32[32,128]{1,0:T(8,128)} %refs_4_.1, s32[3,32,128]{2,1,0:T(8,128)} %refs_5_.1), custom_call_target="tpu_custom_call" | custom-call | tf_op jit(solution)/shard_map/pallas_call | solution.py:595
  34.5 0.7 %shard_map.102 = (f32[4,32,128]{2,1,0:T(8,128)}, f32[4,32,128]{2,1,0:T(8,128)}, f32[4,32,128]{2,1,0:T(8,128)}, f32[4,32,128]{2,1,0:T(8,128)}, f32[32,128]{1,0:T(8,128)}) custom-call(f32[17,32,128]{2,1,0:T(8,128)S(1)} %shard_map.101.result), custom_call_target="tpu_custom_call" | custom-call | tf_op jit(solution)/shard_map/pallas_call | solution.py:630

commit v9 on v8

--- a/solution.py
+++ b/solution.py
@@ -448,6 +448,10 @@
         UV[V_SE] = jnp.where(half, RINGS[3], RE[0])
         strip(U_SE, V_SE)
 
+    for d in (NORTH, SOUTH):
+        for copy in copies(d):
+            copy.wait_send()
+
     @pl.when(first_column)
     def _():
         eastern_strip()
@@ -544,7 +548,7 @@
             fresh = cells - STEP * (div_x + (flux_up - flux_down))
             result[8 + p] = jnp.where(wet[0] > k, fresh, 0.0)
 
-    for d in range(8):
+    for d in (EAST, WEST, NE, SE, NW, SW):
         if d in (SE, NW):
             @pl.when(earlier[d] | later[d])
             def _():

time: 35.4 us -> 35.4 us (level)
  no operation moved by 1% of the time
where the time goes in v9:
time: 35.4 us; the launch traced here: 35.2 us
  Pallas kernels  34.6 us (98%)
  between operations  0.64 us (2%)
    pallas_call x1, Pallas kernels, step(): pl.pallas_call(body, out_shape=pltpu.VMEM((17, ROWS, COLS), F32), in_spec...  33.8 us
    pallas_call x1, Pallas kernels, step(): pl.pallas_call(deal, out_shape=(levels, levels, levels, levels, plane), i...  0.74 us

profile of v9, /device:TPU:230, one launch (start us, length us, event | category | flops | bytes accessed | tf_op | source)
XLA Modules:
  0.0 35.2 jit_solution(16717957147183624714)
XLA Ops:
  0.6 33.8 %shard_map.101.result = f32[17,32,128]{2,1,0:T(8,128)S(1)} custom-call(f32[4,32,128]{2,1,0:T(8,128)} %refs_0_.1, f32[4,32,128]{2,1,0:T(8,128)} %refs_1_.1, f32[4,32,128]{2,1,0:T(8,128)} %refs_2_.1, f32[4,32,128]{2,1,0:T(8,128)} %refs_3_.1, f32[32,128]{1,0:T(8,128)} %refs_4_.1, s32[3,32,128]{2,1,0:T(8,128)} %refs_5_.1), custom_call_target="tpu_custom_call" | custom-call | tf_op jit(solution)/shard_map/pallas_call | solution.py:599
  34.5 0.7 %shard_map.102 = (f32[4,32,128]{2,1,0:T(8,128)}, f32[4,32,128]{2,1,0:T(8,128)}, f32[4,32,128]{2,1,0:T(8,128)}, f32[4,32,128]{2,1,0:T(8,128)}, f32[32,128]{1,0:T(8,128)}) custom-call(f32[17,32,128]{2,1,0:T(8,128)S(1)} %shard_map.101.result), custom_call_target="tpu_custom_call" | custom-call | tf_op jit(solution)/shard_map/pallas_call | solution.py:634
